TPU v7x, 32 devices: a whole 2x2x4 slice. The times are simulated.
32 devices in a mesh: stator: 8 (over z, y), axial: 4 (over x, core).
Axes of the slice: x: 2, y: 2, z: 4, core: 2. Of those that a mesh axis runs over, the one named last changes fastest.
Arguments:
- coeffs: float32 [32, 32768], P(None, ('stator', 'axial')), may hold values from -6 to 6
- elem_edge: int32 [6, 32768], P(None, ('stator', 'axial')), may hold values from 0 to 1151
- curl_map: float32 [3, 6, 32768], P(None, None, ('stator', 'axial')), may hold values from -1.8 to 1.8
- jacobian: bfloat16 [6, 32, 32768], P(None, None, ('stator', 'axial')), may hold values from -4 to 10, as said below
- flux_fwd: bfloat16 [3, 32, 32768], P(None, None, ('stator', 'axial')), may hold values from -6 to 6
- density: float32 [32768], P(('stator', 'axial')), may hold values from 0.05 to 1
- mortar: float32 [128, 128], replicated, may hold values from -0.5 to 0.5
- gap_peer: int32 [4096, 1], P(('stator', 'axial')), may hold values from 0 to 7; in each aligned block of 128 rows (0 to 127, 128 to 255, ...) at most 32 rows name the same one
- gap_block: int32 [4096], P(('stator', 'axial')), may hold values from 0 to 1
Outputs:
- adjoint: float32 [32, 32768], P(None, ('stator', 'axial'))
- density_grad: float32 [32768], P(('stator', 'axial'))
Inputs may be any that keep to these rules, and one draw needn't show every extreme that they name: `elem_edge`: each entry indexes the device's own 1024 edges followed by the first 128 edges of the next axial slab. `gap_peer`: row s * 4 + b of one device names the stator index whose face meets rotor face block b at sample s; at most 32 rows of one device name the same index, and exactly 32 for some index. `jacobian`: each sample's six components form a symmetric matrix with positive diagonal; each off-diagonal entry is at most 0.41 times the square root of the product of its two diagonal entries, so the matrix is positive definite.
All inputs are finite; a program needn't handle non-finite values.
Results may differ from a plain program's by a relative error of at most 0.0003.
Values sent between devices are 32-bit elements; how exact they have to be, the bound alone decides.
No kernel may reach another device: no remote copies, remote signals or barrier semaphores. Data moves between devices by JAX's collectives and lax.ppermute only.
A program may use at most 64 MiB of HBM per device.

v0:
```python
import math

import jax
import jax.numpy as jnp
from jax import lax
from jax.sharding import PartitionSpec as P

S = 32
GE = 128
GB = 4
QB = 2


PENALTY = 4.0
SIMP_POWER = 3.0


def shifted(value, axis, steps):
    count = lax.axis_size(axis)
    leading, last = (max(0, -steps), min(count, count - steps))
    return lax.ppermute(value, axis, [(source, source + steps) for source in range(leading, last)])


def dft_table(count):
    rows = jnp.arange(count, dtype=jnp.float32)[:, None]
    index = jnp.arange(count, dtype=jnp.int32)
    harmonic = ((index + 1) // 2).astype(jnp.float32)[None, :]
    is_sine = ((index % 2 == 0) & (index > 0))[None, :]
    angle = 2.0 * math.pi * harmonic * rows / count
    table = jnp.where(is_sine, jnp.sin(angle), jnp.cos(angle))
    return table * jnp.float32(math.sqrt(2.0 / count))


def element_work(extended, elem_edge, curl_map, jacobian, flux_fwd, density):
    samples = extended.shape[0]
    values = extended[:, elem_edge]
    flux_lam = jnp.einsum("cke,ske->cse", curl_map, values, precision=lax.Precision.HIGHEST)
    jac = jacobian.astype(jnp.float32)
    field_h = jnp.stack(
        [
            jac[0] * flux_lam[0] + jac[3] * flux_lam[1] + jac[4] * flux_lam[2],
            jac[3] * flux_lam[0] + jac[1] * flux_lam[1] + jac[5] * flux_lam[2],
            jac[4] * flux_lam[0] + jac[5] * flux_lam[1] + jac[2] * flux_lam[2],
        ]
    )
    element_terms = jnp.einsum("cke,cse->kes", curl_map, field_h, precision=lax.Precision.HIGHEST)
    summed = jax.ops.segment_sum(
        element_terms.reshape(-1, samples), elem_edge.reshape(-1), num_segments=extended.shape[1]
    )
    energy = jnp.sum(flux_lam * flux_fwd.astype(jnp.float32), axis=(0, 1))
    grad = SIMP_POWER * density * density * energy / samples
    return (summed.T, grad)


def on_device(
    coeffs, elem_edge, curl_map, jacobian, flux_fwd, density, mortar, gap_peer, gap_block
):
    stators = lax.axis_size("stator")
    capacity = 2 * S * GB // stators
    edge_count = coeffs.shape[1]
    face_count = edge_count // 8
    table = dft_table(S)
    in_time = jnp.dot(table, coeffs, precision=lax.Precision.HIGHEST)
    upper_rim = shifted(in_time[:, :face_count], "axial", -1)
    extended = jnp.concatenate([in_time, upper_rim], 1)
    res_ext, density_grad = element_work(extended, elem_edge, curl_map, jacobian, flux_fwd, density)
    lower_rim = shifted(res_ext[:, edge_count:], "axial", 1)
    residual = res_ext[:, :edge_count]
    residual = residual.at[:, :face_count].add(lower_rim)
    rotor_start = edge_count - GB * GE
    rotor_rows = in_time[:, rotor_start:].reshape(S * GB, GE)
    stator_rows = in_time[:, face_count : face_count + QB * GE].reshape(S * QB, GE)
    mapped = jnp.dot(stator_rows, mortar, precision=lax.Precision.HIGHEST)
    owners = gap_peer[:, 0]
    target = (jnp.arange(S, dtype=jnp.int32)[:, None] * QB + gap_block.reshape(S, GB)).reshape(-1)
    onehot = (owners[:, None] == jnp.arange(stators, dtype=jnp.int32)[None, :]).astype(jnp.int32)
    before = jnp.cumsum(onehot, 0) - onehot
    slot_index = jnp.sum(before * onehot, 1)
    places = owners * capacity + slot_index
    slot_vals = (
        jnp.zeros((stators * capacity, GE), jnp.float32)
        .at[places]
        .set(rotor_rows)
        .reshape(stators, capacity, GE)
    )
    slot_keys = (
        jnp.zeros((stators * capacity,), jnp.int32)
        .at[places]
        .set(target + 1)
        .reshape(stators, capacity)
    )
    values_in = lax.all_to_all(slot_vals, "stator", split_axis=0, concat_axis=0, tiled=True)
    keys_in = lax.all_to_all(slot_keys, "stator", split_axis=0, concat_axis=0, tiled=True)
    usable = keys_in > 0
    lookup_rows = jnp.maximum(keys_in - 1, 0)
    jump_rows = jnp.where(usable[..., None], values_in - mapped[lookup_rows], 0.0)
    returned = lax.all_to_all(
        PENALTY * jump_rows, "stator", split_axis=0, concat_axis=0, tiled=True
    )
    returned, jump_slots, lookup_slots = (returned, jump_rows, lookup_rows)
    rotor_term = returned.reshape(stators * capacity, GE)[places]
    own_jumps = jax.ops.segment_sum(
        jump_slots.reshape(-1, GE), lookup_slots.reshape(-1), num_segments=S * QB
    )
    stator_term = -PENALTY * jnp.dot(own_jumps, mortar.T, precision=lax.Precision.HIGHEST)
    residual = residual.at[:, rotor_start:].add(rotor_term.reshape(S, GB * GE))
    residual = residual.at[:, face_count : face_count + QB * GE].add(
        stator_term.reshape(S, QB * GE)
    )
    adjoint = jnp.dot(table.T, residual, precision=lax.Precision.HIGHEST)
    return (adjoint, density_grad)


def solution(mesh):
    placed = (
        P(None, ("stator", "axial")),
        P(None, ("stator", "axial")),
        P(None, None, ("stator", "axial")),
        P(None, None, ("stator", "axial")),
        P(None, None, ("stator", "axial")),
        P(("stator", "axial")),
        P(),
        P(("stator", "axial"), None),
        P(("stator", "axial")),
    )
    return jax.shard_map(
        on_device,
        mesh=mesh,
        in_specs=placed,
        out_specs=(P(None, ("stator", "axial")), P(("stator", "axial"))),
        check_vma=False,
    )
```

profile of v0, /device:TPU:0, one launch (start us, length us, event | category | flops | bytes accessed | tf_op | source)
XLA Modules:
  0.0 136.9 jit_solution(11658341751068461903)
XLA Ops:
  3.9 1.0 scatter_custom_fusion.1
  5.6 7.3 %all-to-all-start = ((s32[8,1,32]{2,1,0:T(1,128)}), s32[8,1,32]{2,1,0:T(1,128)S(1)}, u32[]{:S(2)}, u32[]{:S(2)}) async-start(s32[8,1,32]{2,1,0:T(1,128)} %all_to_all.12), calls=%async_computation | async-start | bytes 8192 | tf_op jit(solution)/shard_map/all_to_all | solution.py:93
  13.5 1.3 collective-permute-start
  15.6 1.0 fusion.37
  16.6 1.4 reshape.223
  18.0 2.0 %convert_element_type.19 = f32[6,32,1024]{2,1,0:T(8,128)} convert(bf16[6,32,1024]{2,1,0:T(8,128)(2,1)} %param.18) | non-fusion elementwise | flops 196608 | bytes 1179648 | tf_op jit(solution)/shard_map/convert_element_type | solution.py:38
  20.0 1.6 %copy.98 = f32[3,6,1024]{1,0,2:T(4,128)S(1)} copy(f32[3,6,1024]{2,1,0:T(8,128)} %param.17) | data formatting | bytes 147456 | tf_op args[2]
  21.6 1.5 %scatter_custom_fusion.2 = f32[256,128]{1,0:T(8,128)} fusion(s32[128]{0:T(128)S(1)} %fusion.30, f32[128,128]{1,0:T(8,128)S(1)} %reshape.241, f32[]{:T(128)} %constant.143.clone.1), kind=kCustom, calls=%fused_computation.34 | custom fusion | bytes 131076 | tf_op jit(solution)/shard_map/scatter | solution.py:83
  24.5 6.0 %all-to-all-start.1 = ((f32[8,32,128]{2,1,0:T(8,128)}), f32[8,32,128]{2,1,0:T(8,128)}, u32[]{:S(2)}, u32[]{:S(2)}) async-start(f32[8,32,128]{2,1,0:T(8,128)} %bitcast.11), calls=%async_computation.1 | async-start | bytes 262144 | tf_op jit(solution)/shard_map/all_to_all | solution.py:92
  31.6 20.9 %gather_fusion = f32[6144,32]{1,0:T(8,128)} fusion(f32[32,1152]{0,1:T(8,128)S(1)} %copy.96, s32[6144]{0:T(1024)S(1)} %broadcast_clamp_fusion), kind=kCustom, calls=%fused_computation | custom fusion | bytes 1597440 | tf_op jit(solution)/shard_map/gather | solution.py:36
  52.5 11.5 %fusion = f32[1024,32,3]{1,2,0:T(4,128)} fusion(f32[3,6,1024]{1,0,2:T(4,128)S(1)} %copy.98, f32[6,1024,32]{2,1,0:T(8,128)} %bitcast.38), kind=kOutput, calls=%fused_computation.7 | convolution fusion | flops 7077888 | bytes 1253376 | tf_op jit(solution)/shard_map/cke,ske->cse/dot_general | solution.py:37
  64.0 1.8 %copy.99 = f32[1024,32,3]{0,1,2:T(8,128)S(1)} copy(f32[1024,32,3]{1,2,0:T(4,128)} %fusion) | data formatting | bytes 786432 | tf_op jit(solution)/shard_map/cke,ske->cse/dot_general | solution.py:37
  65.9 1.8 %copy.100 = f32[3,32,1024]{1,0,2:T(4,128)} copy(f32[3,32,1024]{2,1,0:T(8,128)S(1)} %pad_maximum_fusion) | data formatting | bytes 786432 | tf_op jit(solution)/shard_map/stack | solution.py:39
  67.7 10.0 %convolution_bitcast_fusion = f32[6,1024,32]{2,0,1:T(8,128)S(1)} fusion(f32[3,32,1024]{1,0,2:T(4,128)} %copy.100, f32[3,6,1024]{1,0,2:T(4,128)S(1)} %copy.98), kind=kOutput, calls=%fused_computation.10 | convolution fusion | flops 7077888 | bytes 1253376 | tf_op jit(solution)/shard_map/cke,cse->kes/dot_general | solution.py:46
  78.4 34.4 %scatter_custom_fusion = f32[1152,32]{1,0:T(8,128)} fusion(s32[6144]{0:T(1024)} %reshape.223, f32[6144,32]{1,0:T(8,128)S(1)} %bitcast.41, f32[]{:T(128)} %constant.143.clone.1), kind=kCustom, calls=%fused_computation.14 | custom fusion | flops 196608 | bytes 147968 | tf_op jit(solution)/shard_map/scatter-add | solution.py:47
  112.8 0.8 slice.144
  113.7 1.1 slice.142
  114.7 2.8 %collective-permute-start.1 = (f32[32,128]{0,1:T(8,128)S(1)}, f32[32,128]{0,1:T(8,128)S(1)}, u32[]{:S(2)}, u32[]{:S(2)}) collective-permute-start(f32[32,128]{0,1:T(8,128)S(1)} %slice.144), channel_id=1, source_target_pairs={{0,1},{1,2},{2,3},{4,5},{5,6},{6,7},{8,9},{9,10},{10,11},{12,13},{... | collective-permute-start | bytes 49160 | tf_op jit(solution)/shard_map/ppermute | solution.py:21
  118.1 1.7 %broadcast_multiply_fusion = (f32[8,32,128]{2,1,0:T(8,128)}, f32[8,32,128]{2,1,0:T(8,128)S(1)}) fusion(f32[8,32,128]{2,1,0:T(8,128)} %all-to-all-done.1, f32[8,32,128]{2,1,0:T(8,128)S(1)} %bitcast.45, pred[8,32]{1,0:T(8,128)(4,1)S(1)} %compare_bitcast_fusion), kind=kLoop, calls=%fused_computation.33 | loop fusion | flops 98304 | bytes 524544 | tf_op jit(solution)/shard_map/mul | solution.py:98
  119.8 5.7 %all-to-all-start.2 = ((f32[8,32,128]{2,1,0:T(8,128)}), f32[8,32,128]{2,1,0:T(8,128)S(1)}, u32[]{:S(2)}, u32[]{:S(2)}) async-start(f32[8,32,128]{2,1,0:T(8,128)} %get-tuple-element.38), calls=%async_computation.2 | async-start | bytes 262144 | tf_op jit(solution)/shard_map/all_to_all | solution.py:97
  125.5 1.5 %fusion.12 = f32[32,1024]{0,1:T(8,128)S(1)} fusion(f32[32,1024]{0,1:T(8,128)S(1)} %slice.142, f32[32,128]{0,1:T(8,128)S(1)} %collective-permute-done.1, f32[32,1152]{0,1:T(8,128)} %bitcast.44, pred[]{:T(512)} %compare_reduce_fusion.1), kind=kLoop, calls=%fused_computation.32 | loop fusion | flops 8192 | bytes 147457 | tf_op jit(solution)/shard_map/scatter-add | solution.py:69
  127.0 1.6 %scatter_custom_fusion.3 = f32[64,128]{1,0:T(8,128)S(1)} fusion(s32[256]{0:T(256)} %copy-done.5, f32[256,128]{1,0:T(8,128)S(1)} %bitcast.46, f32[]{:T(128)} %constant.143.clone.1), kind=kCustom, calls=%fused_computation.39 | custom fusion | flops 32768 | bytes 33280 | tf_op jit(solution)/shard_map/scatter-add | solution.py:102
  128.9 4.3 %all-to-all-done.2 = f32[8,32,128]{2,1,0:T(8,128)S(1)} async-done(((f32[8,32,128]{2,1,0:T(8,128)}), f32[8,32,128]{2,1,0:T(8,128)S(1)}, u32[]{:S(2)}, u32[]{:S(2)}) %all-to-all-start.2) | async-done | bytes 131104 | tf_op jit(solution)/shard_map/all_to_all | solution.py:97
  134.8 2.1 %fusion.18 = f32[32,1024]{1,0:T(8,128)} fusion(f32[32,1024]{0,1:T(8,128)S(1)} %fusion.6, f32[32]{0:T(128)} %copy-done.6, pred[32]{0:T(512)(128)(4,1)} %copy-done.7), kind=kOutput, calls=%fused_computation.42 | convolution fusion | flops 12587008 | bytes 262304 | tf_op jit(solution)/shard_map/dot_general | solution.py:110
  (63 shorter events, 11.0 us)
Async XLA Ops:
  0.6 12.3 %copy-start = (f32[32,1024]{1,0:T(8,128)S(1)}, f32[32,1024]{1,0:T(8,128)}, u32[]{:S(2)}) copy-start(f32[32,1024]{1,0:T(8,128)} %param.15) | copy-start | bytes 393220
  5.6 18.9 %all-to-all-start = ((s32[8,1,32]{2,1,0:T(1,128)}), s32[8,1,32]{2,1,0:T(1,128)S(1)}, u32[]{:S(2)}, u32[]{:S(2)}) async-start(s32[8,1,32]{2,1,0:T(1,128)} %all_to_all.12), calls=%async_computation | async-start | bytes 8192 | tf_op jit(solution)/shard_map/all_to_all | solution.py:93
  12.9 0.6 copy-start.6
  12.9 0.5 copy-start.7
  13.5 17.9 %collective-permute-start = (f32[32,128]{1,0:T(8,128)S(1)}, f32[32,128]{1,0:T(8,128)S(1)}, u32[]{:S(2)}, u32[]{:S(2)}) collective-permute-start(f32[32,128]{1,0:T(8,128)S(1)} %slice.133), channel_id=1, source_target_pairs={{1,0},{2,1},{3,2},{5,4},{6,5},{7,6},{9,8},{10,9},{11,10},{13,12},{... | collective-permute-start | bytes 49160 | tf_op jit(solution)/shard_map/ppermute | solution.py:21
  24.5 93.6 %all-to-all-start.1 = ((f32[8,32,128]{2,1,0:T(8,128)}), f32[8,32,128]{2,1,0:T(8,128)}, u32[]{:S(2)}, u32[]{:S(2)}) async-start(f32[8,32,128]{2,1,0:T(8,128)} %bitcast.11), calls=%async_computation.1 | async-start | bytes 262144 | tf_op jit(solution)/shard_map/all_to_all | solution.py:92
  30.6 0.7 copy-start.5
  52.5 13.3 %copy-start.1 = (f32[6,32,1024]{2,1,0:T(8,128)S(1)}, f32[6,32,1024]{2,1,0:T(8,128)}, u32[]{:S(2)}) copy-start(f32[6,32,1024]{2,1,0:T(8,128)} %convert_element_type.19) | copy-start | bytes 2359300
  67.7 10.1 %copy-start.3 = (bf16[3,32,1024]{2,1,0:T(8,128)(2,1)S(1)}, bf16[3,32,1024]{2,1,0:T(8,128)(2,1)}, u32[]{:S(2)}) copy-start(bf16[3,32,1024]{2,1,0:T(8,128)(2,1)} %param.19) | copy-start | bytes 589828
  77.8 39.7 %copy-start.4 = (f32[1024]{0:T(1024)S(1)}, f32[1024]{0:T(1024)}, u32[]{:S(2)}) copy-start(f32[1024]{0:T(1024)} %param.20) | copy-start | bytes 12292
  77.8 50.8 %copy-start.2 = (f32[128,128]{1,0:T(8,128)S(1)}, f32[128,128]{1,0:T(8,128)}, u32[]{:S(2)}) copy-start(f32[128,128]{1,0:T(8,128)} %param.21) | copy-start | bytes 196612
  114.7 10.8 %collective-permute-start.1 = (f32[32,128]{0,1:T(8,128)S(1)}, f32[32,128]{0,1:T(8,128)S(1)}, u32[]{:S(2)}, u32[]{:S(2)}) collective-permute-start(f32[32,128]{0,1:T(8,128)S(1)} %slice.144), channel_id=1, source_target_pairs={{0,1},{1,2},{2,3},{4,5},{5,6},{6,7},{8,9},{9,10},{10,11},{12,13},{... | collective-permute-start | bytes 49160 | tf_op jit(solution)/shard_map/ppermute | solution.py:21
  119.8 13.5 %all-to-all-start.2 = ((f32[8,32,128]{2,1,0:T(8,128)}), f32[8,32,128]{2,1,0:T(8,128)S(1)}, u32[]{:S(2)}, u32[]{:S(2)}) async-start(f32[8,32,128]{2,1,0:T(8,128)} %get-tuple-element.38), calls=%async_computation.2 | async-start | bytes 262144 | tf_op jit(solution)/shard_map/all_to_all | solution.py:97
where the time goes:
time: 138 us; the launch traced here: 137 us
  other arithmetic  47.9 us (35%)
  local copies, waits for them, and re-layouts  35.4 us (26%)
  matrix products  25.2 us (18%)
  starting transfers between devices  23.1 us (17%)
  waiting for transfers between devices  4.36 us (3%)
    scatter-add x1, other arithmetic, element_work(): jax.ops.segment_sum(element_terms.reshape(-1, samples), elem_edge.reshape...  34.4 us
    gather x1, local copies, waits for them, and re-layouts, element_work(): values = extended[:, elem_edge]  20.9 us
    dot_general x1, matrix products, element_work(): jnp.einsum('cke,ske->cse', curl_map, values, precision=lax.Precision.HIGH...  11.5 us
    dot_general x1, matrix products, element_work(): jnp.einsum('cke,cse->kes', curl_map, field_h, precision=lax.Precision.HIG...  10 us
    all_to_all x1, starting transfers between devices, on_device(): lax.all_to_all(slot_keys, 'stator', split_axis=0, concat_axis=0, tiled=True)  7.31 us
    all_to_all x1, starting transfers between devices, on_device(): lax.all_to_all(slot_vals, 'stator', split_axis=0, concat_axis=0, tiled=True)  6 us
    all_to_all x1, starting transfers between devices, on_device(): lax.all_to_all(PENALTY * jump_rows, 'stator', split_axis=0, concat_axis=0...  5.72 us
    all_to_all x1, waiting for transfers between devices, on_device(): lax.all_to_all(PENALTY * jump_rows, 'stator', split_axis=0, concat_axis=0...  4.35 us
  transfers between devices with their start and end apart: 5, of which 1 were waited for; matrix products, arithmetic and copies ran while one was open for 73% of the time, Pallas kernels for 0%

commit v1 on v0

v1 whole, which is shorter than its diff:
```python
import functools
import math

import jax
import jax.numpy as jnp
import numpy as np
from jax import lax
from jax.experimental import pallas as pl
from jax.experimental.pallas import tpu as pltpu
from jax.sharding import PartitionSpec as P

GE = 128
QB = 2
LANES = 128
WIDE = 256
KEY_ROWS = 8

PENALTY = 4.0
SIMP_POWER = 3.0

BF = jnp.bfloat16
F32 = jnp.float32


def shifted(value, axis, steps):
    count = lax.axis_size(axis)
    leading, last = (max(0, -steps), min(count, count - steps))
    return lax.ppermute(value, axis, [(source, source + steps) for source in range(leading, last)])


def dft_table(count):
    rows = np.arange(count, dtype=np.float64)[:, None]
    index = np.arange(count)
    harmonic = ((index + 1) // 2)[None, :]
    is_sine = ((index % 2 == 0) & (index > 0))[None, :]
    angle = 2.0 * math.pi * harmonic * rows / count
    return np.where(is_sine, np.sin(angle), np.cos(angle)) * math.sqrt(2.0 / count)


def table_parts(table):
    high = table.astype(BF)
    low = (table - high.astype(np.float64)).astype(BF)
    return np.concatenate([high, high, low, low], 1)


def split(value):
    high = value.astype(BF)
    low = (value - high.astype(F32)).astype(BF)
    return high, low


def dot(left, right):
    return jnp.dot(left, right, preferred_element_type=F32)


def dot_t(left, right):
    return lax.dot_general(left, right, (((1,), (1,)), ((), ())), preferred_element_type=F32)


def apply_table(table, value):
    high, low = split(value)
    return dot(table, jnp.concatenate([high, low, high, low], 0))


def iota(shape, dim):
    return lax.broadcasted_iota(jnp.int32, shape, dim)


def sorted_rows(peer_ref, block_ref, samples, blocks):
    rows = samples * blocks
    old, new = iota((rows, rows), 0), iota((rows, rows), 1)
    move = jnp.where(old == (new % samples) * blocks + new // samples, 1.0, 0.0).astype(BF)
    both = jnp.concatenate([peer_ref[...], block_ref[...]], 0).astype(F32)
    both = jnp.concatenate([both, jnp.zeros((6, rows), F32)], 0).astype(BF)
    moved = dot(both, move)
    return moved[0:1], moved[1:2]


def gap_kernel(
    samples, stators, blocks, face, rotor_start, table_ref, coeffs_ref, mortar_ref, peer_ref, block_ref,
    send_ref, mapped_ref,
):
    rows = samples * blocks
    slots = 2 * rows
    capacity = slots // stators
    table = table_ref[...]
    face_time = apply_table(table, coeffs_ref[:, face : face + QB * GE])
    rotor_time = apply_table(table, coeffs_ref[:, rotor_start : rotor_start + blocks * GE])
    faces = jnp.concatenate([face_time[:, q * GE : (q + 1) * GE] for q in range(QB)], 0)
    rotors = jnp.concatenate([rotor_time[:, b * GE : (b + 1) * GE] for b in range(blocks)], 0)
    mortar_high, mortar_low = split(mortar_ref[...])
    face_high, face_low = split(faces)
    mapped = dot(
        jnp.concatenate([face_high, face_low, face_high], 1),
        jnp.concatenate([mortar_high, mortar_high, mortar_low], 0),
    )
    mapped_ref[...] = mapped
    peers, chosen = sorted_rows(peer_ref, block_ref, samples, blocks)
    across = jnp.broadcast_to(peers, (rows, rows))
    down = jnp.transpose(across)
    ahead = (across == down) & (iota((rows, rows), 0) < iota((rows, rows), 1))
    rank = jnp.sum(jnp.where(ahead, 1.0, 0.0), 0, keepdims=True)
    place = peers * capacity + rank
    slot = iota((slots, rows), 0).astype(F32)
    pick = jnp.where(slot == place, 1.0, 0.0).astype(BF)
    rotor_high, rotor_low = split(rotors)
    picked = dot(pick, jnp.concatenate([rotor_high, rotor_low], 1))
    packed = picked[:, :GE] + picked[:, GE:]
    key = chosen * samples + (iota((1, rows), 1) % samples).astype(F32) + 1.0
    keys = dot_t(jnp.broadcast_to(key, (KEY_ROWS, rows)).astype(BF), pick)
    for p in range(stators):
        send_ref[p, 0:capacity, :] = packed[p * capacity : (p + 1) * capacity]
        start = p * capacity
        part = keys[:, start // LANES * LANES : (start // LANES + 1) * LANES]
        turn = (LANES - start % LANES) % LANES
        if turn:
            part = pltpu.roll(part, turn, 1)
        send_ref[p, capacity : capacity + KEY_ROWS, :] = part
        send_ref[p, capacity + KEY_ROWS :, :] = mapped


def element_kernel(
    face, rotor_start, table_ref, back_ref, coeffs_ref, rim_ref, edge_ref, curl_ref, jac_ref, fwd_ref, density_ref,
    adjoint_ref, rim_out_ref, grad_ref,
):
    samples, edges = coeffs_ref.shape
    elements = edge_ref.shape[1]
    table = table_ref[...]
    own_time = apply_table(table, coeffs_ref[...])
    rim_time = apply_table(table, rim_ref[...])
    extended = [own_time[:, i * LANES : (i + 1) * LANES] for i in range(edges // LANES)]
    extended += [rim_time[:, i * LANES : (i + 1) * LANES] for i in range(face // LANES)]
    total = edges + face
    wides = -(-total // WIDE)
    places = iota((WIDE, LANES), 0).astype(F32).astype(BF)
    summed = jnp.zeros((wides * 2 * samples, WIDE), F32)
    for chunk in range(elements // WIDE):
        lefts, rights = [], []
        left_lanes = [[] for _ in range(6)]
        right_lanes = [[] for _ in range(6)]
        for half in range(WIDE // LANES):
            start = chunk * WIDE + half * LANES
            lanes = slice(start, start + LANES)
            values = []
            index_rows = edge_ref[:, lanes]
            for m in range(6):
                index = index_rows[m : m + 1]
                low = jnp.broadcast_to(index & (LANES - 1), (samples, LANES))
                high = jnp.broadcast_to(index // LANES, (samples, LANES))
                found = [
                    jnp.take_along_axis(part, low, axis=1, mode="promise_in_bounds") for part in extended
                ]
                bit = 1
                while len(found) > 1:
                    odd = (high & bit) != 0
                    found = [
                        jnp.where(odd, found[i + 1], found[i]) if i + 1 < len(found) else found[i]
                        for i in range(0, len(found), 2)
                    ]
                    bit *= 2
                values.append(found[0])
            curl = [[curl_ref[c, m : m + 1, lanes] for m in range(6)] for c in range(3)]
            flux = []
            for c in range(3):
                acc = curl[c][0] * values[0]
                for m in range(1, 6):
                    acc = acc + curl[c][m] * values[m]
                flux.append(acc)
            energy = flux[0] * fwd_ref[0, :, lanes].astype(F32)
            for c in range(1, 3):
                energy = energy + flux[c] * fwd_ref[c, :, lanes].astype(F32)
            energy = jnp.sum(energy, 0, keepdims=True)
            density = density_ref[:, lanes]
            grad_ref[:, lanes] = SIMP_POWER * density * density * energy / samples
            jac = [jac_ref[k, :, lanes].astype(F32) for k in range(6)]
            field = [
                jac[0] * flux[0] + jac[3] * flux[1] + jac[4] * flux[2],
                jac[3] * flux[0] + jac[1] * flux[1] + jac[5] * flux[2],
                jac[4] * flux[0] + jac[5] * flux[1] + jac[2] * flux[2],
            ]
            for m in range(6):
                term = curl[0][m] * field[0] + curl[1][m] * field[1] + curl[2][m] * field[2]
                high, low = split(term)
                pair = jnp.concatenate([high, low], 0)
                index = index_rows[m : m + 1]
                wide = jnp.broadcast_to(index // WIDE, (16, LANES)).astype(F32).astype(BF)
                wide = jnp.concatenate([wide] * (2 * samples // 16), 0)
                left_lanes[m].append(
                    jnp.concatenate([jnp.where(wide == w, pair, jnp.zeros_like(pair)) for w in range(wides)], 0)
                )
                place = jnp.broadcast_to(index & (WIDE - 1), (16, LANES)).astype(F32).astype(BF)
                place = jnp.concatenate([place] * (WIDE // 16), 0)
                right_lanes[m].append(jnp.where(place == places, jnp.ones_like(place), jnp.zeros_like(place)))
        left = jnp.concatenate([part for m in range(6) for part in left_lanes[m]], 1)
        right = jnp.concatenate([part for m in range(6) for part in right_lanes[m]], 1)
        summed = summed + dot_t(left, right)
    pieces = []
    for w in range(wides):
        base = w * 2 * samples
        pieces.append(summed[base : base + samples] + summed[base + samples : base + 2 * samples])
    residual = jnp.concatenate(pieces, 1)
    own = jnp.concatenate(
        [residual[:, :rotor_start], residual[:, rotor_start:edges] + PENALTY * own_time[:, rotor_start:]], 1
    )
    back = back_ref[...]
    adjoint_ref[...] = apply_table(back, own)
    rim_out_ref[...] = apply_table(back, residual[:, edges:total])


def join_kernel(
    samples, stators, blocks, face, rotor_start, back_ref, adjoint_ref, rim_ref, got_ref, mapped_ref, mortar_ref,
    peer_ref, block_ref, out_ref,
):
    rows = samples * blocks
    slots = 2 * rows
    capacity = slots // stators
    faces_at = capacity + KEY_ROWS
    peers, chosen = sorted_rows(peer_ref, block_ref, samples, blocks)
    wanted = (peers * QB + chosen) * samples + (iota((1, rows), 1) % samples).astype(F32)
    wanted = jnp.transpose(jnp.broadcast_to(wanted, (LANES, rows)))
    face_rows = stators * QB * samples
    select = jnp.concatenate(
        [
            jnp.where(wanted == (iota((rows, LANES), 1) + at).astype(F32), 1.0, 0.0).astype(BF)
            for at in range(0, face_rows, LANES)
        ],
        1,
    )
    faces = jnp.concatenate([got_ref[p, faces_at:, :] for p in range(stators)], 0)
    face_high, face_low = split(faces)
    facing = dot(select, jnp.concatenate([face_high, face_low], 1))
    facing = facing[:, :GE] + facing[:, GE:]
    rotor_term = jnp.concatenate(
        [facing[b * samples : (b + 1) * samples] for b in range(blocks)], 1
    ) * (-PENALTY)

    lane = iota((KEY_ROWS, LANES), 1)
    key_parts = []
    for v in range(slots // LANES):
        acc = jnp.zeros((KEY_ROWS, LANES), F32)
        for p in range(v * LANES // capacity, (v + 1) * LANES // capacity):
            part = jnp.where(lane < capacity, got_ref[p, capacity:faces_at, :], 0.0)
            turn = p * capacity % LANES
            acc = acc + (pltpu.roll(part, turn, 1) if turn else part)
        key_parts.append(acc[0:1])
    key = jnp.concatenate(key_parts, 1)
    targets = QB * samples
    hit = jnp.where(key == (iota((targets, slots), 0) + 1).astype(F32), 1.0, 0.0)
    count = jnp.sum(hit, 1, keepdims=True)
    packed = jnp.concatenate([got_ref[p, 0:capacity, :] for p in range(stators)], 0)
    packed_high, packed_low = split(packed)
    gathered = dot(hit.astype(BF), jnp.concatenate([packed_high, packed_low], 1))
    gathered = gathered[:, :GE] + gathered[:, GE:] - count * mapped_ref[...]
    mortar_high, mortar_low = split(mortar_ref[...])
    gathered_high, gathered_low = split(gathered)
    stator_term = dot_t(
        jnp.concatenate([gathered_high, gathered_low, gathered_high], 1),
        jnp.concatenate([mortar_high, mortar_high, mortar_low], 1),
    ) * (-PENALTY)
    stator_term = jnp.concatenate([stator_term[q * samples : (q + 1) * samples] for q in range(QB)], 1)
    back = back_ref[...]
    out_ref[...] = adjoint_ref[...]
    out_ref[:, :face] += rim_ref[...]
    out_ref[:, face : face + QB * GE] += apply_table(back, stator_term)
    out_ref[:, rotor_start : rotor_start + blocks * GE] += apply_table(back, rotor_term)


def on_device(coeffs, elem_edge, curl_map, jacobian, flux_fwd, density, mortar, gap_peer, gap_block):
    stators = lax.axis_size("stator")
    samples, edges = coeffs.shape
    rows = gap_block.shape[0]
    blocks = rows // samples
    capacity = 2 * rows // stators
    face = edges // 8
    rotor_start = edges - blocks * GE
    elements = density.shape[0]
    table_value = dft_table(samples)
    table = jnp.asarray(table_parts(table_value))
    back = jnp.asarray(table_parts(table_value.T))
    peer = gap_peer.reshape(1, rows)
    block = gap_block.reshape(1, rows)

    rim = shifted(coeffs[:, :face], "axial", -1)
    send_shape = (stators, capacity + KEY_ROWS + QB * samples, GE)
    send, mapped = pl.pallas_call(
        functools.partial(gap_kernel, samples, stators, blocks, face, rotor_start),
        out_shape=(jax.ShapeDtypeStruct(send_shape, F32), jax.ShapeDtypeStruct((QB * samples, GE), F32)),
        name="gap_send",
    )(table, coeffs, mortar, peer, block)
    got = lax.all_to_all(send, "stator", split_axis=0, concat_axis=0, tiled=True)
    adjoint, rim_out, grad = pl.pallas_call(
        functools.partial(element_kernel, face, rotor_start),
        out_shape=(
            jax.ShapeDtypeStruct((samples, edges), F32),
            jax.ShapeDtypeStruct((samples, face), F32),
            jax.ShapeDtypeStruct((1, elements), F32),
        ),
        name="element",
    )(table, back, coeffs, rim, elem_edge, curl_map, jacobian, flux_fwd, density.reshape(1, elements))
    lower = shifted(rim_out, "axial", 1)
    adjoint = pl.pallas_call(
        functools.partial(join_kernel, samples, stators, blocks, face, rotor_start),
        out_shape=jax.ShapeDtypeStruct((samples, edges), F32),
        name="join",
    )(back, adjoint, lower, got, mapped, mortar, peer, block)
    return adjoint, grad.reshape(elements)


def solution(mesh):
    placed = (
        P(None, ("stator", "axial")),
        P(None, ("stator", "axial")),
        P(None, None, ("stator", "axial")),
        P(None, None, ("stator", "axial")),
        P(None, None, ("stator", "axial")),
        P(("stator", "axial")),
        P(),
        P(("stator", "axial"), None),
        P(("stator", "axial")),
    )
    return jax.shard_map(
        on_device,
        mesh=mesh,
        in_specs=placed,
        out_specs=(P(None, ("stator", "axial")), P(("stator", "axial"))),
        check_vma=False,
    )
```

time: 138 us -> 28.4 us (0.21)
  other arithmetic: 47.9 us -> 0 us
  local copies, waits for them, and re-layouts: 35.4 us -> 2.08 us
  matrix products: 25.2 us -> 0 us
  starting transfers between devices: 23.1 us -> 12.6 us
  Pallas kernels: 0 us -> 9.87 us
  waiting for transfers between devices: 4.36 us -> 2.81 us
    scatter-add x5 -> x0, other arithmetic: 38.2 us -> none  [the longest x1 34.4 us: element_work(): jax.ops.segment_sum(element_terms.reshape(-1, samples), elem_edge.reshape...]
    dot_general x6 -> x0, matrix products: 25.2 us -> none  [the longest x1 11.5 us: element_work(): jnp.einsum('cke,ske->cse', curl_map, values, precision=lax.Precision.HIGH...]
    gather x3 -> x0, local copies, waits for them, and re-layouts: 22.3 us -> none  [the longest x1 20.9 us: element_work(): values = extended[:, elem_edge]]
    all_to_all x3 -> x1, starting transfers between devices: 19 us -> 7.31 us  [on_device(): lax.all_to_all(send, 'stator', split_axis=0, concat_axis=0, tiled=True)]
    pallas_call x0 -> x3, Pallas kernels: none -> 9.87 us  [the longest x1 5.24 us: on_device(): pl.pallas_call(functools.partial(element_kernel, face, rotor_start), out_...]
    all_to_all x3 -> x1, waiting for transfers between devices: 4.35 us -> 0.01 us  [on_device(): lax.all_to_all(send, 'stator', split_axis=0, concat_axis=0, tiled=True)]
    another operation x6 -> x0, local copies, waits for them, and re-layouts: 3.38 us -> none  [the longest x1 1.77 us: element_work(): jnp.stack([jac[0] * flux_lam[0] + jac[3] * flux_lam[1] + jac[4] * flux_la...]
    ppermute x2, waiting for transfers between devices: 0.01 us -> 2.81 us  [shifted(): lax.ppermute(value, axis, [(source, source + steps) for source in range(l...]
  transfers between devices with their start and end apart: 5 -> 3, of which waited for: 1 -> 2; matrix products, arithmetic and copies ran while one was open for 73% -> 3% of each run, Pallas kernels for 0% -> 19%
where the time goes in v1:
time: 28.4 us; the launch traced here: 28 us
  starting transfers between devices  12.6 us (44%)
  Pallas kernels  9.87 us (35%)
  waiting for transfers between devices  2.81 us (10%)
  local copies, waits for them, and re-layouts  2.08 us (7%)
  between operations  0.65 us (2%)
    all_to_all x1, starting transfers between devices, on_device(): lax.all_to_all(send, 'stator', split_axis=0, concat_axis=0, tiled=True)  7.31 us
    ppermute x2, starting transfers between devices, shifted(): lax.ppermute(value, axis, [(source, source + steps) for source in range(l...  5.32 us
    pallas_call x1, Pallas kernels, on_device(): pl.pallas_call(functools.partial(element_kernel, face, rotor_start), out_...  5.24 us
    ppermute x2, waiting for transfers between devices, shifted(): lax.ppermute(value, axis, [(source, source + steps) for source in range(l...  2.81 us
    pallas_call x1, Pallas kernels, on_device(): pl.pallas_call(functools.partial(gap_kernel, samples, stators, blocks, fa...  2.32 us
    pallas_call x1, Pallas kernels, on_device(): pl.pallas_call(functools.partial(join_kernel, samples, stators, blocks, f...  2.31 us
    unnamed x6, local copies, waits for them, and re-layouts  1.36 us
    slice x1, local copies, waits for them, and re-layouts, on_device(): rim = shifted(coeffs[:, :face], 'axial', -1)  0.72 us
  transfers between devices with their start and end apart: 3, of which 2 were waited for; matrix products, arithmetic and copies ran while one was open for 3% of the time, Pallas kernels for 19%

profile of v1, /device:TPU:0, one launch (start us, length us, event | category | flops | bytes accessed | tf_op | source)
XLA Modules:
  0.0 28.0 jit_solution(17093559567305443075)
XLA Ops:
  0.6 2.3 %gap_send.1 = (f32[8,104,128]{2,1,0:T(8,128)}, f32[64,128]{1,0:T(8,128)}) custom-call(bf16[32,128]{1,0:T(8,128)(2,1)} %constant.4.clone.table_ref, f32[32,1024]{1,0:T(8,128)} %coeffs_ref.3, f32[128,128]{1,0:T(8,128)} %mortar_ref.3, s32[1,128]{1,0:T(1,128)} %bitcast.5, s32[1,128]{1,0:T(1,128)} %bitcast.7), custom_call_target="tpu_custom_call" | custom-call | tf_op jit(solution)/shard_map/gap_send/pallas_call | solution.py:285
  3.0 7.3 %all-to-all-start = ((f32[8,104,128]{2,1,0:T(8,128)}), f32[8,104,128]{2,1,0:T(8,128)S(1)}, u32[]{:S(2)}, u32[]{:S(2)}) async-start(f32[8,104,128]{2,1,0:T(8,128)} %get-tuple-element.9), calls=%async_computation | async-start | bytes 851968 | tf_op jit(solution)/shard_map/all_to_all | solution.py:290
  10.3 0.7 %slice.3 = f32[32,128]{1,0:T(8,128)S(1)} slice(f32[32,1024]{1,0:T(8,128)} %coeffs_ref.3), slice={[0:32], [0:128]} | slice | bytes 32768 | tf_op jit(solution)/shard_map/slice | solution.py:283
  11.0 1.3 %collective-permute-start = (f32[32,128]{1,0:T(8,128)S(1)}, f32[32,128]{1,0:T(8,128)S(1)}, u32[]{:S(2)}, u32[]{:S(2)}) collective-permute-start(f32[32,128]{1,0:T(8,128)S(1)} %slice.3), channel_id=1, source_target_pairs={{1,0},{2,1},{3,2},{5,4},{6,5},{7,6},{9,8},{10,9},{11,10},{13,12},{... | collective-permute-start | bytes 49160 | tf_op jit(solution)/shard_map/ppermute | solution.py:28
  12.3 1.8 %collective-permute-done.rim_ref = f32[32,128]{1,0:T(8,128)S(1)} collective-permute-done((f32[32,128]{1,0:T(8,128)S(1)}, f32[32,128]{1,0:T(8,128)S(1)}, u32[]{:S(2)}, u32[]{:S(2)}) %collective-permute-start) | collective-permute-done | bytes 16416 | tf_op jit(solution)/shard_map/ppermute | solution.py:28
  14.0 0.0 copy-start.1
  14.0 0.6 %copy-done.1 = f32[32,128]{1,0:T(8,128)} copy-done((f32[32,128]{1,0:T(8,128)}, f32[32,128]{1,0:T(8,128)S(1)}, u32[]{:S(2)}) %copy-start.1) | copy-done | bytes 16408
  14.7 5.2 %element.1 = (f32[32,1024]{1,0:T(8,128)}, f32[32,128]{1,0:T(8,128)}, f32[1,1024]{1,0:T(1,128)}) custom-call(bf16[32,128]{1,0:T(8,128)(2,1)} %constant.4.clone.table_ref, bf16[32,128]{1,0:T(8,128)(2,1)} %constant.5.clone.back_ref, f32[32,1024]{1,0:T(8,128)} %coeffs_ref.3, f32[32,128]{1,0:T(8,128)} %copy-done.1, s32[6,1024]{1,0:T(8,128)} %edge_ref.1, ...), custom_call_target="tpu_custom_call" | custom-call | tf_op jit(solution)/shard_map/element/pallas_call | solution.py:291
  19.9 4.0 %collective-permute-start.1 = (f32[32,128]{1,0:T(8,128)}, f32[32,128]{1,0:T(8,128)S(1)}, u32[]{:S(2)}, u32[]{:S(2)}) collective-permute-start(f32[32,128]{1,0:T(8,128)} %get-tuple-element.8), channel_id=1, source_target_pairs={{0,1},{1,2},{2,3},{4,5},{5,6},{6,7},{8,9},{9,10},{10,11},{12,13},{... | collective-permute-start | bytes 49160 | tf_op jit(solution)/shard_map/ppermute | solution.py:28
  23.9 1.0 %collective-permute-done.1.rim_ref = f32[32,128]{1,0:T(8,128)S(1)} collective-permute-done((f32[32,128]{1,0:T(8,128)}, f32[32,128]{1,0:T(8,128)S(1)}, u32[]{:S(2)}, u32[]{:S(2)}) %collective-permute-start.1) | collective-permute-done | bytes 16416 | tf_op jit(solution)/shard_map/ppermute | solution.py:28
  25.0 0.0 copy-start.2
  25.0 0.0 all-to-all-done.got_ref
  25.0 0.0 copy-start
  25.0 0.6 %copy-done.2 = f32[32,128]{1,0:T(8,128)} copy-done((f32[32,128]{1,0:T(8,128)}, f32[32,128]{1,0:T(8,128)S(1)}, u32[]{:S(2)}) %copy-start.2) | copy-done | bytes 16408
  25.6 0.2 copy-done
  25.7 2.3 %join.1 = f32[32,1024]{1,0:T(8,128)} custom-call(bf16[32,128]{1,0:T(8,128)(2,1)} %constant.5.clone.back_ref, f32[32,1024]{1,0:T(8,128)} %get-tuple-element.7.adjoint_ref, f32[32,128]{1,0:T(8,128)} %copy-done.2, f32[8,104,128]{2,1,0:T(8,128)} %copy-done, f32[64,128]{1,0:T(8,128)} %get-tuple-element.10.mapped_ref, f32[128,128]{1,0:T(8,128)} %mortar_ref.3, ...), custom_call_target="tpu_custom_call" | custom-call | tf_op jit(solution)/shard_map/join/pallas_call | solution.py:301
Async XLA Ops:
  3.0 22.0 %all-to-all-start = ((f32[8,104,128]{2,1,0:T(8,128)}), f32[8,104,128]{2,1,0:T(8,128)S(1)}, u32[]{:S(2)}, u32[]{:S(2)}) async-start(f32[8,104,128]{2,1,0:T(8,128)} %get-tuple-element.9), calls=%async_computation | async-start | bytes 851968 | tf_op jit(solution)/shard_map/all_to_all | solution.py:290
  11.0 3.1 %collective-permute-start = (f32[32,128]{1,0:T(8,128)S(1)}, f32[32,128]{1,0:T(8,128)S(1)}, u32[]{:S(2)}, u32[]{:S(2)}) collective-permute-start(f32[32,128]{1,0:T(8,128)S(1)} %slice.3), channel_id=1, source_target_pairs={{1,0},{2,1},{3,2},{5,4},{6,5},{7,6},{9,8},{10,9},{11,10},{13,12},{... | collective-permute-start | bytes 49160 | tf_op jit(solution)/shard_map/ppermute | solution.py:28
  14.0 0.6 %copy-start.1 = (f32[32,128]{1,0:T(8,128)}, f32[32,128]{1,0:T(8,128)S(1)}, u32[]{:S(2)}) copy-start(f32[32,128]{1,0:T(8,128)S(1)} %collective-permute-done.rim_ref) | copy-start | bytes 49156
  19.9 5.1 %collective-permute-start.1 = (f32[32,128]{1,0:T(8,128)}, f32[32,128]{1,0:T(8,128)S(1)}, u32[]{:S(2)}, u32[]{:S(2)}) collective-permute-start(f32[32,128]{1,0:T(8,128)} %get-tuple-element.8), channel_id=1, source_target_pairs={{0,1},{1,2},{2,3},{4,5},{5,6},{6,7},{8,9},{9,10},{10,11},{12,13},{... | collective-permute-start | bytes 49160 | tf_op jit(solution)/shard_map/ppermute | solution.py:28
  25.0 0.6 %copy-start.2 = (f32[32,128]{1,0:T(8,128)}, f32[32,128]{1,0:T(8,128)S(1)}, u32[]{:S(2)}) copy-start(f32[32,128]{1,0:T(8,128)S(1)} %collective-permute-done.1.rim_ref) | copy-start | bytes 49156
  25.0 0.8 %copy-start = (f32[8,104,128]{2,1,0:T(8,128)}, f32[8,104,128]{2,1,0:T(8,128)S(1)}, u32[]{:S(2)}) copy-start(f32[8,104,128]{2,1,0:T(8,128)S(1)} %all-to-all-done.got_ref) | copy-start | bytes 1277956

commit v2 on v1

v2 whole, which is shorter than its diff:
```python
import functools
import math

import jax
import jax.numpy as jnp
import numpy as np
from jax import lax
from jax.experimental import pallas as pl
from jax.experimental.pallas import tpu as pltpu
from jax.sharding import PartitionSpec as P

GE = 128
QB = 2
LANES = 128
WIDE = 256
CHUNK = 256
LOOK = (1, 3, 5)
NEAR_BYTES = 1 << 20

PENALTY = 4.0
SIMP_POWER = 3.0

BF = jnp.bfloat16
F32 = jnp.float32


def shifted(value, axis, steps):
    count = lax.axis_size(axis)
    leading, last = (max(0, -steps), min(count, count - steps))
    return lax.ppermute(value, axis, [(source, source + steps) for source in range(leading, last)])


def dft_table(count):
    rows = np.arange(count, dtype=np.float64)[:, None]
    index = np.arange(count)
    harmonic = ((index + 1) // 2)[None, :]
    is_sine = ((index % 2 == 0) & (index > 0))[None, :]
    angle = 2.0 * math.pi * harmonic * rows / count
    return np.where(is_sine, np.sin(angle), np.cos(angle)) * math.sqrt(2.0 / count)


def table_parts(table):
    high = table.astype(BF)
    low = (table - high.astype(np.float64)).astype(BF)
    return np.concatenate([high, high, low, low], 1)


def split(value):
    high = value.astype(BF)
    low = (value - high.astype(F32)).astype(BF)
    return high, low


def dot(left, right):
    return jnp.dot(left, right, preferred_element_type=F32)


def dot_t(left, right):
    return lax.dot_general(left, right, (((1,), (1,)), ((), ())), preferred_element_type=F32)


def apply_table(table, value):
    high, low = split(value)
    return dot(table, jnp.concatenate([high, low, high, low], 0))


def iota(shape, dim):
    return lax.broadcasted_iota(jnp.int32, shape, dim)


def sorted_rows(peer_ref, block_ref, samples, blocks):
    rows = samples * blocks
    old, new = iota((rows, rows), 0), iota((rows, rows), 1)
    move = jnp.where(old == (new % samples) * blocks + new // samples, 1.0, 0.0).astype(BF)
    both = jnp.concatenate([peer_ref[...], block_ref[...]], 0).astype(F32)
    both = jnp.concatenate([both, jnp.zeros((6, rows), F32)], 0).astype(BF)
    moved = dot(both, move)
    return moved[0:1], moved[1:2]


def gap_kernel(
    samples, stators, blocks, face, rotor_start, table_ref, coeffs_ref, mortar_ref, peer_ref, block_ref,
    send_ref, turned_ref, rim_ref,
):
    rows = samples * blocks
    slots = 2 * rows
    capacity = slots // stators
    face_rows = QB * samples
    rim_ref[...] = coeffs_ref[:, :face]
    table = table_ref[...]
    face_time = apply_table(table, coeffs_ref[:, face : face + QB * GE])
    rotor_time = apply_table(table, coeffs_ref[:, rotor_start : rotor_start + blocks * GE])
    faces = jnp.concatenate([face_time[:, q * GE : (q + 1) * GE] for q in range(QB)], 0)
    rotors = jnp.concatenate([rotor_time[:, b * GE : (b + 1) * GE] for b in range(blocks)], 0)
    mortar_high, mortar_low = split(mortar_ref[...])
    mortar_down = jnp.concatenate([mortar_high, mortar_high, mortar_low], 0)
    mortar_across = jnp.concatenate([mortar_high, mortar_high, mortar_low], 1)

    def triple(value):
        high, low = split(value)
        return jnp.concatenate([high, low, high], 1)

    mapped = dot(triple(faces), mortar_down)
    turned_ref[...] = dot_t(triple(mapped), mortar_across)
    rotor_turned = dot_t(triple(rotors), mortar_across)
    peers, chosen = sorted_rows(peer_ref, block_ref, samples, blocks)
    across = jnp.broadcast_to(peers, (rows, rows))
    down = jnp.transpose(across)
    ahead = (across == down) & (iota((rows, rows), 0) < iota((rows, rows), 1))
    rank = jnp.sum(jnp.where(ahead, 1.0, 0.0), 0, keepdims=True)
    place = peers * capacity + rank
    slot = iota((slots, rows), 0).astype(F32)
    pick = jnp.where(slot == place, 1.0, 0.0).astype(BF)
    rotor_high, rotor_low = split(rotor_turned)
    picked = dot(pick, jnp.concatenate([rotor_high, rotor_low], 1))
    packed = picked[:, :GE] + picked[:, GE:]
    key = chosen * samples + (iota((1, rows), 1) % samples).astype(F32) + 1.0
    keys = dot_t(jnp.broadcast_to(key, (8, rows)).astype(BF), pick)
    for p in range(stators):
        first = p * (face_rows + capacity + 1)
        send_ref[first : first + face_rows, :] = mapped
        first += face_rows
        send_ref[first : first + capacity, :] = packed[p * capacity : (p + 1) * capacity]
        first += capacity
        start = p * capacity
        part = keys[:, start // LANES * LANES : (start // LANES + 1) * LANES]
        turn = (LANES - start % LANES) % LANES
        if turn:
            part = pltpu.roll(part, turn, 1)
        send_ref[first : first + 1, :] = part[:1]


def choose_kernel(samples, stators, blocks, wide_ref, peer_ref, block_ref, after_ref, out_ref):
    rows = samples * blocks
    pairs = stators * QB
    wanted = (peer_ref[...] * QB + block_ref[...]).astype(F32)
    wanted = jnp.broadcast_to(wanted, (8, rows)).astype(BF)
    lane = iota((rows, LANES), 1) % samples
    row = iota((rows, LANES), 0)
    spread = jnp.concatenate(
        [jnp.where(row == lane * blocks + b, 1.0, 0.0).astype(BF) for b in range(blocks)], 1
    )
    wanted = dot(wanted, spread)
    each = LANES // samples
    owner = (iota((samples, LANES), 1) // samples).astype(F32)
    for piece in range(2):
        values = wide_ref[piece * samples : (piece + 1) * samples, :].astype(F32)
        for b in range(blocks):
            want = jnp.broadcast_to(wanted[0:1, b * LANES : (b + 1) * LANES], (samples, LANES))
            for v in range(pairs // each):
                out_ref[(piece * blocks + b) * samples : (piece * blocks + b + 1) * samples,
                        v * LANES : (v + 1) * LANES] = jnp.where(want == owner + v * each, values, 0.0).astype(BF)


def element_kernel(
    face, rotor_start, table_ref, back_ref, coeffs_ref, rim_ref, edge_ref, curl_ref, jac_ref, fwd_ref, density_ref,
    adjoint_ref, rim_out_ref, grad_ref,
):
    samples, edges = coeffs_ref.shape
    elements = edge_ref.shape[1]
    table = table_ref[...]
    own_time = apply_table(table, coeffs_ref[...])
    rim_time = apply_table(table, rim_ref[:, :face])
    total = edges + face
    wides = -(-total // WIDE)
    whole = jnp.concatenate([own_time, rim_time], 1)
    extended = [whole[:, i * LANES : (i + 1) * LANES] for i in range(total // LANES)]
    padded = jnp.concatenate([whole, jnp.zeros((samples, wides * WIDE - total), F32)], 1)
    stack = jnp.concatenate(
        [part for w in range(wides) for part in split(padded[:, w * WIDE : (w + 1) * WIDE])], 0
    )
    places = iota((WIDE, LANES), 0).astype(F32).astype(BF)
    summed = jnp.zeros((wides * 2 * samples, WIDE), F32)
    for chunk in range(elements // CHUNK):
        lane_slices = [
            slice(chunk * CHUNK + half * LANES, chunk * CHUNK + (half + 1) * LANES) for half in range(CHUNK // LANES)
        ]
        rights = []
        for m in range(6):
            parts = []
            for lanes in lane_slices:
                index = edge_ref[m : m + 1, lanes]
                place = jnp.broadcast_to(index & (WIDE - 1), (16, LANES)).astype(F32).astype(BF)
                place = jnp.concatenate([place] * (WIDE // 16), 0)
                parts.append(jnp.where(place == places, jnp.ones_like(place), jnp.zeros_like(place)))
            rights.append(jnp.concatenate(parts, 1))
        looked = {m: dot(stack, rights[m]) for m in LOOK}
        left_lanes = [[] for _ in range(6)]
        for half, lanes in enumerate(lane_slices):
            at = slice(half * LANES, (half + 1) * LANES)
            values = []
            for m in range(6):
                index = edge_ref[m : m + 1, lanes]
                if m in LOOK:
                    found = [
                        looked[m][2 * w * samples : (2 * w + 1) * samples, at]
                        + looked[m][(2 * w + 1) * samples : (2 * w + 2) * samples, at]
                        for w in range(wides)
                    ]
                    high = jnp.broadcast_to(index // WIDE, (samples, LANES))
                else:
                    low = jnp.broadcast_to(index & (LANES - 1), (samples, LANES))
                    found = [
                        jnp.take_along_axis(part, low, axis=1, mode="promise_in_bounds") for part in extended
                    ]
                    high = jnp.broadcast_to(index // LANES, (samples, LANES))
                bit = 1
                while len(found) > 1:
                    odd = (high & bit) != 0
                    found = [
                        jnp.where(odd, found[i + 1], found[i]) if i + 1 < len(found) else found[i]
                        for i in range(0, len(found), 2)
                    ]
                    bit *= 2
                values.append(found[0])
            curl = [[curl_ref[c, m : m + 1, lanes] for m in range(6)] for c in range(3)]
            flux = []
            for c in range(3):
                acc = curl[c][0] * values[0]
                for m in range(1, 6):
                    acc = acc + curl[c][m] * values[m]
                flux.append(acc)
            energy = flux[0] * fwd_ref[0, :, lanes].astype(F32)
            for c in range(1, 3):
                energy = energy + flux[c] * fwd_ref[c, :, lanes].astype(F32)
            energy = jnp.sum(energy, 0, keepdims=True)
            density = density_ref[:, lanes]
            grad_ref[:, lanes] = SIMP_POWER * density * density * energy / samples
            jac = [jac_ref[k, :, lanes].astype(F32) for k in range(6)]
            field = [
                jac[0] * flux[0] + jac[3] * flux[1] + jac[4] * flux[2],
                jac[3] * flux[0] + jac[1] * flux[1] + jac[5] * flux[2],
                jac[4] * flux[0] + jac[5] * flux[1] + jac[2] * flux[2],
            ]
            for m in range(6):
                term = curl[0][m] * field[0] + curl[1][m] * field[1] + curl[2][m] * field[2]
                high, low = split(term)
                pair = jnp.concatenate([high, low], 0)
                index = edge_ref[m : m + 1, lanes]
                wide = jnp.broadcast_to(index // WIDE, (16, LANES)).astype(F32).astype(BF)
                wide = jnp.concatenate([wide] * (2 * samples // 16), 0)
                left_lanes[m].append(
                    jnp.concatenate([jnp.where(wide == w, pair, jnp.zeros_like(pair)) for w in range(wides)], 0)
                )
        left = jnp.concatenate([part for m in range(6) for part in left_lanes[m]], 1)
        summed = summed + dot_t(left, jnp.concatenate(rights, 1))
    pieces = []
    for w in range(wides):
        base = w * 2 * samples
        pieces.append(summed[base : base + samples] + summed[base + samples : base + 2 * samples])
    residual = jnp.concatenate(pieces, 1)
    own = jnp.concatenate(
        [residual[:, :rotor_start], residual[:, rotor_start:edges] + PENALTY * own_time[:, rotor_start:]], 1
    )
    back = back_ref[...]
    adjoint_ref[...] = apply_table(back, own)
    rim_out_ref[...] = apply_table(back, residual[:, edges:total])


def join_kernel(
    samples, stators, blocks, face, rotor_start, back_ref, adjoint_ref, rim_ref, got_ref, turned_ref, choose_ref,
    out_ref,
):
    slots = 2 * samples * blocks
    capacity = slots // stators
    face_rows = QB * samples
    keys_at = face_rows + capacity
    each = keys_at + 1
    faces = jnp.concatenate([got_ref[p * each : p * each + face_rows, :] for p in range(stators)], 0)
    face_high, face_low = split(faces)
    facing = dot(choose_ref[...], jnp.concatenate([face_high, face_low], 1))
    rows = blocks * samples
    facing = (facing[:rows, :GE] + facing[:rows, GE:]) + (facing[rows:, :GE] + facing[rows:, GE:])

    lane = iota((1, LANES), 1)
    key_parts = []
    for v in range(slots // LANES):
        acc = jnp.zeros((1, LANES), F32)
        for p in range(v * LANES // capacity, (v + 1) * LANES // capacity):
            part = jnp.where(lane < capacity, got_ref[p * each + keys_at : (p + 1) * each, :], 0.0)
            turn = p * capacity % LANES
            acc = acc + (pltpu.roll(part, turn, 1) if turn else part)
        key_parts.append(acc[0:1])
    key = jnp.concatenate(key_parts, 1)
    hit = jnp.where(key == (iota((face_rows, slots), 0) + 1).astype(F32), 1.0, 0.0)
    count = jnp.sum(hit, 1, keepdims=True)
    packed = jnp.concatenate([got_ref[p * each + face_rows : p * each + keys_at, :] for p in range(stators)], 0)
    packed_high, packed_low = split(packed)
    gathered = dot(hit.astype(BF), jnp.concatenate([packed_high, packed_low], 1))
    gathered = (gathered[:, :GE] + gathered[:, GE:] - count * turned_ref[...]) * (-PENALTY)
    stator_term = jnp.concatenate([gathered[q * samples : (q + 1) * samples] for q in range(QB)], 1)
    stator_term = apply_table(back_ref[...], stator_term)
    out_ref[:, :face] = adjoint_ref[:, :face] + rim_ref[...]
    out_ref[:, face : face + QB * GE] = adjoint_ref[:, face : face + QB * GE] + stator_term
    out_ref[:, face + QB * GE : rotor_start] = adjoint_ref[:, face + QB * GE : rotor_start]
    for b in range(blocks):
        at = slice(rotor_start + b * GE, rotor_start + (b + 1) * GE)
        out_ref[:, at] = adjoint_ref[:, at] + facing[b * samples : (b + 1) * samples]


def small(shape, kind):
    return math.prod(shape) * jnp.dtype(kind).itemsize <= NEAR_BYTES


def call(kernel, near, *shapes):
    spec = lambda inside: pl.BlockSpec(memory_space=pltpu.VMEM) if inside else pl.BlockSpec()

    def run(*operands):
        close = [near and small(operand.shape, operand.dtype) for operand in operands]
        operands = [
            pltpu.with_memory_space_constraint(operand, pltpu.VMEM) if inside else operand
            for inside, operand in zip(close, operands)
        ]
        return pl.pallas_call(
            kernel,
            out_shape=[
                pltpu.VMEM(shape, kind) if inside and small(shape, kind) else jax.ShapeDtypeStruct(shape, kind)
                for inside, shape, kind in shapes
            ],
            in_specs=[spec(inside) for inside in close],
            out_specs=[spec(inside and small(shape, kind)) for inside, shape, kind in shapes],
        )(*operands)

    return run


def on_device(coeffs, elem_edge, curl_map, jacobian, flux_fwd, density, mortar, gap_peer, gap_block):
    stators = lax.axis_size("stator")
    samples, edges = coeffs.shape
    rows = gap_block.shape[0]
    blocks = rows // samples
    capacity = 2 * rows // stators
    face = edges // 8
    rotor_start = edges - blocks * GE
    elements = density.shape[0]
    face_rows = QB * samples
    table_value = dft_table(samples)
    table = jnp.asarray(table_parts(table_value))
    back = jnp.asarray(table_parts(table_value.T))
    wide = -PENALTY * table_value.T
    wide_high = wide.astype(BF)
    wide_low = (wide - wide_high.astype(np.float64)).astype(BF)
    wide = jnp.asarray(np.tile(np.concatenate([wide_high, wide_low], 0), (1, LANES // samples)))
    peer = gap_peer.reshape(1, rows)
    block = gap_block.reshape(1, rows)
    send, turned, rim = call(
        functools.partial(gap_kernel, samples, stators, blocks, face, rotor_start),
        False,
        (False, (stators * (face_rows + capacity + 1), GE), F32),
        (True, (face_rows, GE), F32),
        (True, (samples, face), F32),
    )(table, coeffs, mortar, peer, block)
    rim = shifted(rim, "axial", -1)
    parts = send.reshape(stators, face_rows + capacity + 1, 1, GE)
    got = lax.all_to_all(parts, "stator", split_axis=0, concat_axis=0, tiled=True).reshape(send.shape)
    adjoint, rim_out, grad = call(
        functools.partial(element_kernel, face, rotor_start),
        True,
        (True, (samples, edges), F32),
        (True, (samples, face), F32),
        (False, (1, elements), F32),
    )(table, back, coeffs, rim, elem_edge, curl_map, jacobian, flux_fwd, density.reshape(1, elements))
    lower = shifted(rim_out, "axial", 1)
    (choose,) = call(
        functools.partial(choose_kernel, samples, stators, blocks), True, (True, (2 * rows, stators * face_rows), BF)
    )(wide, peer, block, rim_out)
    (adjoint,) = call(
        functools.partial(join_kernel, samples, stators, blocks, face, rotor_start),
        True,
        (False, (samples, edges), F32),
    )(back, adjoint, lower, got, turned, choose)
    return adjoint, grad.reshape(elements)


def solution(mesh):
    placed = (
        P(None, ("stator", "axial")),
        P(None, ("stator", "axial")),
        P(None, None, ("stator", "axial")),
        P(None, None, ("stator", "axial")),
        P(None, None, ("stator", "axial")),
        P(("stator", "axial")),
        P(),
        P(("stator", "axial"), None),
        P(("stator", "axial")),
    )
    return jax.shard_map(
        on_device,
        mesh=mesh,
        in_specs=placed,
        out_specs=(P(None, ("stator", "axial")), P(("stator", "axial"))),
        check_vma=False,
    )
```

time: 28.4 us -> 23.8 us (0.84)
  Pallas kernels: 9.87 us -> 6.88 us
  local copies, waits for them, and re-layouts: 2.08 us -> 0.06 us
  starting transfers between devices: 12.6 us -> 12.9 us
    pallas_call x3 -> x4, Pallas kernels: 9.87 us -> 6.88 us  [run(): pl.pallas_call(kernel, out_shape=[pltpu.VMEM(shape, kind) if inside and s...]
    unnamed x6 -> x22, local copies, waits for them, and re-layouts: 1.36 us -> 0.06 us
    slice x1 -> x0, local copies, waits for them, and re-layouts: 0.72 us -> none  [on_device(): rim = shifted(coeffs[:, :face], 'axial', -1)]
    all_to_all x1, waiting for transfers between devices: 0.01 us -> 0.46 us  [on_device(): lax.all_to_all(parts, 'stator', split_axis=0, concat_axis=0, tiled=True)]
    ppermute x2, waiting for transfers between devices: 2.81 us -> 2.39 us  [shifted(): lax.ppermute(value, axis, [(source, source + steps) for source in range(l...]
  transfers between devices with their start and end apart: 3 -> 3, of which waited for: 2 -> 3; matrix products, arithmetic and copies ran while one was open for 3% -> 0% of each run, Pallas kernels for 19% -> 14%
where the time goes in v2:
time: 23.8 us; the launch traced here: 23.5 us
  starting transfers between devices  12.9 us (54%)
  Pallas kernels  6.88 us (29%)
  waiting for transfers between devices  2.85 us (12%)
  between operations  0.78 us (3%)
    all_to_all x1, starting transfers between devices, on_device(): lax.all_to_all(parts, 'stator', split_axis=0, concat_axis=0, tiled=True)  7.45 us
    pallas_call x4, Pallas kernels, run(): pl.pallas_call(kernel, out_shape=[pltpu.VMEM(shape, kind) if inside and s...  6.88 us
    ppermute x2, starting transfers between devices, shifted(): lax.ppermute(value, axis, [(source, source + steps) for source in range(l...  5.47 us
    ppermute x2, waiting for transfers between devices, shifted(): lax.ppermute(value, axis, [(source, source + steps) for source in range(l...  2.39 us
  transfers between devices with their start and end apart: 3, of which 3 were waited for; matrix products, arithmetic and copies ran while one was open for 0% of the time, Pallas kernels for 14%

profile of v2, /device:TPU:0, one launch (start us, length us, event | category | flops | bytes accessed | tf_op | source)
XLA Modules:
  0.0 23.5 jit_solution(13671790522307229119)
XLA Ops:
  0.6 0.0 copy-start.3
  0.6 2.5 %shard_map.131 = (f32[776,128]{1,0:T(8,128)}, f32[64,128]{1,0:T(8,128)S(1)}, f32[32,128]{1,0:T(8,128)S(1)}) custom-call(bf16[32,128]{1,0:T(8,128)(2,1)} %constant.6.clone.table_ref, f32[32,1024]{1,0:T(8,128)} %coeffs_ref.3, f32[128,128]{1,0:T(8,128)} %mortar_ref.1, s32[1,128]{1,0:T(1,128)} %bitcast.8, s32[1,128]{1,0:T(1,128)} %bitcast.10), custom_call_target="tpu_custom_call" | custom-call | tf_op jit(solution)/shard_map/pallas_call | solution.py:314
  3.2 0.0 copy-start.5
  3.2 0.0 copy-start.6
  3.2 0.0 copy-start.8
  3.2 7.5 %all-to-all-start = ((f32[8,97,1,128]{3,2,1,0:T(1,128)}), f32[8,97,1,128]{3,2,1,0:T(1,128)S(1)}, u32[]{:S(2)}, u32[]{:S(2)}) async-start(f32[8,97,1,128]{3,2,1,0:T(1,128)} %bitcast.12), calls=%async_computation | async-start | bytes 794624 | tf_op jit(solution)/shard_map/all_to_all | solution.py:355
  10.7 1.3 %collective-permute-start = (f32[32,128]{1,0:T(8,128)S(1)}, f32[32,128]{1,0:T(8,128)S(1)}, u32[]{:S(2)}, u32[]{:S(2)}) collective-permute-start(f32[32,128]{1,0:T(8,128)S(1)} %get-tuple-element.8), channel_id=1, source_target_pairs={{1,0},{2,1},{3,2},{5,4},{6,5},{7,6},{9,8},{10,9},{11,10},{13,12},{... | collective-permute-start | bytes 49160 | tf_op jit(solution)/shard_map/ppermute | solution.py:30
  12.0 1.8 %collective-permute-done.rim_ref = f32[32,128]{1,0:T(8,128)S(1)} collective-permute-done((f32[32,128]{1,0:T(8,128)S(1)}, f32[32,128]{1,0:T(8,128)S(1)}, u32[]{:S(2)}, u32[]{:S(2)}) %collective-permute-start) | collective-permute-done | bytes 16416 | tf_op jit(solution)/shard_map/ppermute | solution.py:30
  13.7 0.0 copy-done.3
  13.7 0.0 copy-done
  13.7 0.0 copy-done.1
  13.7 0.0 copy-done.2
  13.8 0.0 copy-done.4
  13.8 0.0 copy-done.5
  13.8 0.0 copy-done.6
  13.8 0.0 copy-done.8
  13.8 0.0 copy-start.7
  13.8 3.1 %shard_map.132 = (f32[32,1024]{1,0:T(8,128)S(1)}, f32[32,128]{1,0:T(8,128)S(1)}, f32[1,1024]{1,0:T(1,128)}) custom-call(bf16[32,128]{1,0:T(8,128)(2,1)S(1)} %copy-done.6, bf16[32,128]{1,0:T(8,128)(2,1)S(1)} %copy-done.4, f32[32,1024]{1,0:T(8,128)S(1)} %copy-done, f32[32,128]{1,0:T(8,128)S(1)} %collective-permute-done.rim_ref, s32[6,1024]{1,0:T(8,128)S(1)} %copy-done.5, ...), custom_call_target="tpu_custom_call" | custom-call | tf_op jit(solution)/shard_map/pallas_call | solution.py:314
  16.9 0.0 copy-start.10
  17.0 4.2 %collective-permute-start.1 = (f32[32,128]{1,0:T(8,128)S(1)}, f32[32,128]{1,0:T(8,128)S(1)}, u32[]{:S(2)}, u32[]{:S(2)}) collective-permute-start(f32[32,128]{1,0:T(8,128)S(1)} %get-tuple-element.10.after_ref), channel_id=1, source_target_pairs={{0,1},{1,2},{2,3},{4,5},{5,6},{6,7},{8,9},{9,10},{10,11},{12,13},{... | collective-permute-start | bytes 49160 | tf_op jit(solution)/shard_map/ppermute | solution.py:30
  21.2 0.2 shard_map.133.choose_ref
  21.4 0.6 %collective-permute-done.1.rim_ref = f32[32,128]{1,0:T(8,128)S(1)} collective-permute-done((f32[32,128]{1,0:T(8,128)S(1)}, f32[32,128]{1,0:T(8,128)S(1)}, u32[]{:S(2)}, u32[]{:S(2)}) %collective-permute-start.1) | collective-permute-done | bytes 16416 | tf_op jit(solution)/shard_map/ppermute | solution.py:30
  22.0 0.5 %all-to-all-done = f32[8,97,1,128]{3,2,1,0:T(1,128)S(1)} async-done(((f32[8,97,1,128]{3,2,1,0:T(1,128)}), f32[8,97,1,128]{3,2,1,0:T(1,128)S(1)}, u32[]{:S(2)}, u32[]{:S(2)}) %all-to-all-start) | async-done | bytes 397344 | tf_op jit(solution)/shard_map/all_to_all | solution.py:355
  22.4 1.0 %shard_map.134 = f32[32,1024]{1,0:T(8,128)} custom-call(bf16[32,128]{1,0:T(8,128)(2,1)S(1)} %copy-done.4, f32[32,1024]{1,0:T(8,128)S(1)} %get-tuple-element.9.adjoint_ref, f32[32,128]{1,0:T(8,128)S(1)} %collective-permute-done.1.rim_ref, f32[776,128]{1,0:T(8,128)S(1)} %bitcast.6, f32[64,128]{1,0:T(8,128)S(1)} %get-tuple-element.12.turned_ref, ...), custom_call_target="tpu_custom_call" | custom-call | tf_op jit(solution)/shard_map/pallas_call | solution.py:314
  (8 shorter events, 0.0 us)
Async XLA Ops:
  0.6 13.1 %copy-start.3 = (f32[3,6,1024]{2,1,0:T(8,128)S(1)}, f32[3,6,1024]{2,1,0:T(8,128)}, u32[]{:S(2)}) copy-start(f32[3,6,1024]{2,1,0:T(8,128)} %curl_ref.1) | copy-start | bytes 221188
  3.2 10.6 %copy-start = (f32[32,1024]{1,0:T(8,128)S(1)}, f32[32,1024]{1,0:T(8,128)}, u32[]{:S(2)}) copy-start(f32[32,1024]{1,0:T(8,128)} %coeffs_ref.3) | copy-start | bytes 393220
  3.2 10.6 %copy-start.1 = (bf16[6,32,1024]{2,1,0:T(8,128)(2,1)S(1)}, bf16[6,32,1024]{2,1,0:T(8,128)(2,1)}, u32[]{:S(2)}) copy-start(bf16[6,32,1024]{2,1,0:T(8,128)(2,1)} %jac_ref.1) | copy-start | bytes 1179652
  3.2 10.6 %copy-start.2 = (bf16[3,32,1024]{2,1,0:T(8,128)(2,1)S(1)}, bf16[3,32,1024]{2,1,0:T(8,128)(2,1)}, u32[]{:S(2)}) copy-start(bf16[3,32,1024]{2,1,0:T(8,128)(2,1)} %fwd_ref.1) | copy-start | bytes 589828
  3.2 10.6 %copy-start.4 = (bf16[32,128]{1,0:T(8,128)(2,1)S(1)}, bf16[32,128]{1,0:T(8,128)(2,1)}, u32[]{:S(2)}) copy-start(bf16[32,128]{1,0:T(8,128)(2,1)} %constant.7.clone.back_ref) | copy-start | bytes 24580
  3.2 10.6 %copy-start.5 = (s32[6,1024]{1,0:T(8,128)S(1)}, s32[6,1024]{1,0:T(8,128)}, u32[]{:S(2)}) copy-start(s32[6,1024]{1,0:T(8,128)} %edge_ref.1) | copy-start | bytes 73732
  3.2 10.6 %copy-start.6 = (bf16[32,128]{1,0:T(8,128)(2,1)S(1)}, bf16[32,128]{1,0:T(8,128)(2,1)}, u32[]{:S(2)}) copy-start(bf16[32,128]{1,0:T(8,128)(2,1)} %constant.6.clone.table_ref) | copy-start | bytes 24580
  3.2 10.6 %copy-start.8 = (f32[1024]{0:T(1024)S(1)}, f32[1024]{0:T(1024)}, u32[]{:S(2)}) copy-start(f32[1024]{0:T(1024)} %param.17) | copy-start | bytes 12292
  3.2 19.2 %all-to-all-start = ((f32[8,97,1,128]{3,2,1,0:T(1,128)}), f32[8,97,1,128]{3,2,1,0:T(1,128)S(1)}, u32[]{:S(2)}, u32[]{:S(2)}) async-start(f32[8,97,1,128]{3,2,1,0:T(1,128)} %bitcast.12), calls=%async_computation | async-start | bytes 794624 | tf_op jit(solution)/shard_map/all_to_all | solution.py:355
  10.7 3.1 %collective-permute-start = (f32[32,128]{1,0:T(8,128)S(1)}, f32[32,128]{1,0:T(8,128)S(1)}, u32[]{:S(2)}, u32[]{:S(2)}) collective-permute-start(f32[32,128]{1,0:T(8,128)S(1)} %get-tuple-element.8), channel_id=1, source_target_pairs={{1,0},{2,1},{3,2},{5,4},{6,5},{7,6},{9,8},{10,9},{11,10},{13,12},{... | collective-permute-start | bytes 49160 | tf_op jit(solution)/shard_map/ppermute | solution.py:30
  13.8 7.4 %copy-start.7 = (bf16[64,128]{1,0:T(8,128)(2,1)S(1)}, bf16[64,128]{1,0:T(8,128)(2,1)}, u32[]{:S(2)}) copy-start(bf16[64,128]{1,0:T(8,128)(2,1)} %constant.8.clone.wide_ref) | copy-start | bytes 49156
  16.9 4.2 %copy-start.9 = (s32[128,1]{0,1:T(1,128)S(1)}, s32[128,1]{0,1:T(1,128)}, u32[]{:S(2)}) copy-start(s32[128,1]{0,1:T(1,128)} %param.19) | copy-start | bytes 1540
  16.9 4.2 %copy-start.10 = (s32[128]{0:T(128)S(1)}, s32[128]{0:T(128)}, u32[]{:S(2)}) copy-start(s32[128]{0:T(128)} %param.20) | copy-start | bytes 1540
  17.0 5.0 %collective-permute-start.1 = (f32[32,128]{1,0:T(8,128)S(1)}, f32[32,128]{1,0:T(8,128)S(1)}, u32[]{:S(2)}, u32[]{:S(2)}) collective-permute-start(f32[32,128]{1,0:T(8,128)S(1)} %get-tuple-element.10.after_ref), channel_id=1, source_target_pairs={{0,1},{1,2},{2,3},{4,5},{5,6},{6,7},{8,9},{9,10},{10,11},{12,13},{... | collective-permute-start | bytes 49160 | tf_op jit(solution)/shard_map/ppermute | solution.py:30

commit v3 on v2

--- a/solution.py
+++ b/solution.py
@@ -68,53 +68,56 @@
     return lax.broadcasted_iota(jnp.int32, shape, dim)
 
 
-def sorted_rows(peer_ref, block_ref, samples, blocks):
-    rows = samples * blocks
-    old, new = iota((rows, rows), 0), iota((rows, rows), 1)
-    move = jnp.where(old == (new % samples) * blocks + new // samples, 1.0, 0.0).astype(BF)
-    both = jnp.concatenate([peer_ref[...], block_ref[...]], 0).astype(F32)
-    both = jnp.concatenate([both, jnp.zeros((6, rows), F32)], 0).astype(BF)
-    moved = dot(both, move)
-    return moved[0:1], moved[1:2]
+def triple(value):
+    high, low = split(value)
+    return jnp.concatenate([high, low, high], 1)
 
 
 def gap_kernel(
-    samples, stators, blocks, face, rotor_start, table_ref, coeffs_ref, mortar_ref, peer_ref, block_ref,
-    send_ref, turned_ref, rim_ref,
+    samples, stators, blocks, face, rotor_start, table_far, coeffs_far, mortar_far, peer_far, block_far,
+    send_ref, mapped_ref, rim_ref, table_ref, coeffs_ref, mortar_ref, peer_ref, block_ref, sems,
 ):
+    fars = (peer_far, block_far, coeffs_far, table_far, mortar_far)
+    nears = (peer_ref, block_ref, coeffs_ref, table_ref, mortar_ref)
+    copies = [pltpu.make_async_copy(far, near, sems.at[i]) for i, (far, near) in enumerate(zip(fars, nears))]
+    for copy in copies:
+        copy.start()
     rows = samples * blocks
     slots = 2 * rows
     capacity = slots // stators
     face_rows = QB * samples
+    old, new = iota((rows, rows), 0), iota((rows, rows), 1)
+    move = jnp.where(old == (new % samples) * blocks + new // samples, 1.0, 0.0).astype(BF)
+    earlier = jnp.where(old < new, 1.0, 0.0)
+    slot = iota((slots, rows), 0).astype(F32)
+    sample = (iota((1, rows), 1) % samples).astype(F32) + 1.0
+    for copy in copies:
+        copy.wait()
+    both = jnp.concatenate([peer_ref[...], block_ref[...]], 0).astype(F32)
+    both = jnp.concatenate([both, jnp.zeros((6, rows), F32)], 0).astype(BF)
+    both = dot(both, move)
+    peers, chosen = both[0:1], both[1:2]
     rim_ref[...] = coeffs_ref[:, :face]
     table = table_ref[...]
+    rotor_time = apply_table(table, coeffs_ref[:, rotor_start : rotor_start + blocks * GE])
     face_time = apply_table(table, coeffs_ref[:, face : face + QB * GE])
-    rotor_time = apply_table(table, coeffs_ref[:, rotor_start : rotor_start + blocks * GE])
+    rotors = jnp.concatenate([rotor_time[:, b * GE : (b + 1) * GE] for b in range(blocks)], 0)
     faces = jnp.concatenate([face_time[:, q * GE : (q + 1) * GE] for q in range(QB)], 0)
-    rotors = jnp.concatenate([rotor_time[:, b * GE : (b + 1) * GE] for b in range(blocks)], 0)
     mortar_high, mortar_low = split(mortar_ref[...])
     mortar_down = jnp.concatenate([mortar_high, mortar_high, mortar_low], 0)
     mortar_across = jnp.concatenate([mortar_high, mortar_high, mortar_low], 1)
-
-    def triple(value):
-        high, low = split(value)
-        return jnp.concatenate([high, low, high], 1)
-
+    rotor_turned = dot_t(triple(rotors), mortar_across)
     mapped = dot(triple(faces), mortar_down)
-    turned_ref[...] = dot_t(triple(mapped), mortar_across)
-    rotor_turned = dot_t(triple(rotors), mortar_across)
-    peers, chosen = sorted_rows(peer_ref, block_ref, samples, blocks)
+    mapped_ref[...] = mapped
     across = jnp.broadcast_to(peers, (rows, rows))
     down = jnp.transpose(across)
-    ahead = (across == down) & (iota((rows, rows), 0) < iota((rows, rows), 1))
-    rank = jnp.sum(jnp.where(ahead, 1.0, 0.0), 0, keepdims=True)
+    rank = jnp.sum(jnp.where(across == down, earlier, 0.0), 0, keepdims=True)
     place = peers * capacity + rank
-    slot = iota((slots, rows), 0).astype(F32)
     pick = jnp.where(slot == place, 1.0, 0.0).astype(BF)
     rotor_high, rotor_low = split(rotor_turned)
     picked = dot(pick, jnp.concatenate([rotor_high, rotor_low], 1))
     packed = picked[:, :GE] + picked[:, GE:]
-    key = chosen * samples + (iota((1, rows), 1) % samples).astype(F32) + 1.0
+    key = chosen * samples + sample
     keys = dot_t(jnp.broadcast_to(key, (8, rows)).astype(BF), pick)
     for p in range(stators):
         first = p * (face_rows + capacity + 1)
@@ -130,7 +133,12 @@
         send_ref[first : first + 1, :] = part[:1]
 
 
-def choose_kernel(samples, stators, blocks, wide_ref, peer_ref, block_ref, after_ref, out_ref):
+def choose_kernel(
+    samples, stators, blocks, wide_ref, peer_ref, block_ref, mapped_ref, mortar_ref, after_ref, out_ref, turned_ref
+):
+    mortar_high, mortar_low = split(mortar_ref[...])
+    mortar_across = jnp.concatenate([mortar_high, mortar_high, mortar_low], 1)
+    turned_ref[...] = dot_t(triple(mapped_ref[...]), mortar_across)
     rows = samples * blocks
     pairs = stators * QB
     wanted = (peer_ref[...] * QB + block_ref[...]).astype(F32)
@@ -302,8 +310,11 @@
     return math.prod(shape) * jnp.dtype(kind).itemsize <= NEAR_BYTES
 
 
-def call(kernel, near, *shapes):
-    spec = lambda inside: pl.BlockSpec(memory_space=pltpu.VMEM) if inside else pl.BlockSpec()
+def call(kernel, near, *shapes, far=(), scratch=()):
+    def spec(inside, anywhere=False):
+        if anywhere:
+            return pl.BlockSpec(memory_space=pl.ANY)
+        return pl.BlockSpec(memory_space=pltpu.VMEM) if inside else pl.BlockSpec()
 
     def run(*operands):
         close = [near and small(operand.shape, operand.dtype) for operand in operands]
@@ -317,9 +328,10 @@
                 pltpu.VMEM(shape, kind) if inside and small(shape, kind) else jax.ShapeDtypeStruct(shape, kind)
                 for inside, shape, kind in shapes
             ],
-            in_specs=[spec(inside) for inside in close],
+            in_specs=[spec(inside) for inside in close] + [spec(False, True)] * len(far),
             out_specs=[spec(inside and small(shape, kind)) for inside, shape, kind in shapes],
-        )(*operands)
+            scratch_shapes=scratch,
+        )(*operands, *far)
 
     return run
 
@@ -343,13 +355,17 @@
     wide = jnp.asarray(np.tile(np.concatenate([wide_high, wide_low], 0), (1, LANES // samples)))
     peer = gap_peer.reshape(1, rows)
     block = gap_block.reshape(1, rows)
-    send, turned, rim = call(
+    ahead = (table, coeffs, mortar, peer, block)
+    send, mapped, rim = call(
         functools.partial(gap_kernel, samples, stators, blocks, face, rotor_start),
         False,
         (False, (stators * (face_rows + capacity + 1), GE), F32),
         (True, (face_rows, GE), F32),
         (True, (samples, face), F32),
-    )(table, coeffs, mortar, peer, block)
+        far=ahead,
+        scratch=[pltpu.VMEM(value.shape, value.dtype) for value in ahead]
+        + [pltpu.SemaphoreType.DMA((len(ahead),))],
+    )()
     rim = shifted(rim, "axial", -1)
     parts = send.reshape(stators, face_rows + capacity + 1, 1, GE)
     got = lax.all_to_all(parts, "stator", split_axis=0, concat_axis=0, tiled=True).reshape(send.shape)
@@ -361,9 +377,12 @@
         (False, (1, elements), F32),
     )(table, back, coeffs, rim, elem_edge, curl_map, jacobian, flux_fwd, density.reshape(1, elements))
     lower = shifted(rim_out, "axial", 1)
-    (choose,) = call(
-        functools.partial(choose_kernel, samples, stators, blocks), True, (True, (2 * rows, stators * face_rows), BF)
-    )(wide, peer, block, rim_out)
+    choose, turned = call(
+        functools.partial(choose_kernel, samples, stators, blocks),
+        True,
+        (True, (2 * rows, stators * face_rows), BF),
+        (True, (face_rows, GE), F32),
+    )(wide, peer, block, mapped, mortar, rim_out)
     (adjoint,) = call(
         functools.partial(join_kernel, samples, stators, blocks, face, rotor_start),
         True,

time: 23.8 us -> 23.6 us (level)
  no operation moved by 1% of the time
where the time goes in v3:
time: 23.6 us; the launch traced here: 23.3 us
  starting transfers between devices  12.9 us (55%)
  Pallas kernels  6.68 us (28%)
  waiting for transfers between devices  2.78 us (12%)
  between operations  0.83 us (4%)
    all_to_all x1, starting transfers between devices, on_device(): lax.all_to_all(parts, 'stator', split_axis=0, concat_axis=0, tiled=True)  7.45 us
    pallas_call x4, Pallas kernels, run(): pl.pallas_call(kernel, out_shape=[pltpu.VMEM(shape, kind) if inside and s...  6.68 us
    ppermute x2, starting transfers between devices, shifted(): lax.ppermute(value, axis, [(source, source + steps) for source in range(l...  5.47 us
    ppermute x2, waiting for transfers between devices, shifted(): lax.ppermute(value, axis, [(source, source + steps) for source in range(l...  2.33 us
  transfers between devices with their start and end apart: 3, of which 3 were waited for; matrix products, arithmetic and copies ran while one was open for 0% of the time, Pallas kernels for 14%

profile of v3, /device:TPU:0, one launch (start us, length us, event | category | flops | bytes accessed | tf_op | source)
XLA Modules:
  0.0 23.3 jit_solution(2914252452359741870)
XLA Ops:
  0.6 0.0 copy-start.4
  0.6 2.3 %shard_map.131 = (f32[776,128]{1,0:T(8,128)}, f32[64,128]{1,0:T(8,128)S(1)}, f32[32,128]{1,0:T(8,128)S(1)}) custom-call(bf16[32,128]{1,0:T(8,128)(2,1)} %constant.6.clone.table_far.table_ref, f32[32,1024]{1,0:T(8,128)} %coeffs_ref.1, f32[128,128]{1,0:T(8,128)} %mortar_ref.1, s32[1,128]{1,0:T(1,128)} %bitcast.8, s32[1,128]{1,0:T(1,128)} %bitcast.10), custom_call_target="tpu_custom_call" | custom-call | tf_op jit(solution)/shard_map/pallas_call | solution.py:325
  2.9 0.0 copy-start
  2.9 0.0 copy-start.1
  3.0 0.0 copy-start.3
  3.0 0.0 copy-start.5
  3.0 0.0 copy-start.6
  3.0 0.0 copy-start.7
  3.0 0.0 copy-start.9
  3.0 7.5 %all-to-all-start = ((f32[8,97,1,128]{3,2,1,0:T(1,128)}), f32[8,97,1,128]{3,2,1,0:T(1,128)S(1)}, u32[]{:S(2)}, u32[]{:S(2)}) async-start(f32[8,97,1,128]{3,2,1,0:T(1,128)} %bitcast.12), calls=%async_computation | async-start | bytes 794624 | tf_op jit(solution)/shard_map/all_to_all | solution.py:371
  10.5 1.3 %collective-permute-start = (f32[32,128]{1,0:T(8,128)S(1)}, f32[32,128]{1,0:T(8,128)S(1)}, u32[]{:S(2)}, u32[]{:S(2)}) collective-permute-start(f32[32,128]{1,0:T(8,128)S(1)} %get-tuple-element.10), channel_id=1, source_target_pairs={{1,0},{2,1},{3,2},{5,4},{6,5},{7,6},{9,8},{10,9},{11,10},{13,12},{... | collective-permute-start | bytes 49160 | tf_op jit(solution)/shard_map/ppermute | solution.py:30
  11.8 1.8 %collective-permute-done.rim_ref = f32[32,128]{1,0:T(8,128)S(1)} collective-permute-done((f32[32,128]{1,0:T(8,128)S(1)}, f32[32,128]{1,0:T(8,128)S(1)}, u32[]{:S(2)}, u32[]{:S(2)}) %collective-permute-start) | collective-permute-done | bytes 16416 | tf_op jit(solution)/shard_map/ppermute | solution.py:30
  13.5 0.0 copy-done.4
  13.5 0.0 copy-done
  13.5 0.0 copy-done.1
  13.6 0.0 copy-start.2
  13.6 0.0 copy-start.8
  13.6 3.1 %shard_map.132 = (f32[32,1024]{1,0:T(8,128)S(1)}, f32[32,128]{1,0:T(8,128)S(1)}, f32[1,1024]{1,0:T(1,128)}) custom-call(bf16[32,128]{1,0:T(8,128)(2,1)S(1)} %copy-done.7, bf16[32,128]{1,0:T(8,128)(2,1)S(1)} %copy-done.5, f32[32,1024]{1,0:T(8,128)S(1)} %copy-done, f32[32,128]{1,0:T(8,128)S(1)} %collective-permute-done.rim_ref, s32[6,1024]{1,0:T(8,128)S(1)} %copy-done.6, ...), custom_call_target="tpu_custom_call" | custom-call | tf_op jit(solution)/shard_map/pallas_call | solution.py:325
  16.8 0.0 copy-start.11
  16.8 4.2 %collective-permute-start.1 = (f32[32,128]{1,0:T(8,128)S(1)}, f32[32,128]{1,0:T(8,128)S(1)}, u32[]{:S(2)}, u32[]{:S(2)}) collective-permute-start(f32[32,128]{1,0:T(8,128)S(1)} %get-tuple-element.12.after_ref), channel_id=1, source_target_pairs={{0,1},{1,2},{2,3},{4,5},{5,6},{6,7},{8,9},{9,10},{10,11},{12,13},{... | collective-permute-start | bytes 49160 | tf_op jit(solution)/shard_map/ppermute | solution.py:30
  21.0 0.2 shard_map.133
  21.2 0.6 %collective-permute-done.1.rim_ref = f32[32,128]{1,0:T(8,128)S(1)} collective-permute-done((f32[32,128]{1,0:T(8,128)S(1)}, f32[32,128]{1,0:T(8,128)S(1)}, u32[]{:S(2)}, u32[]{:S(2)}) %collective-permute-start.1) | collective-permute-done | bytes 16416 | tf_op jit(solution)/shard_map/ppermute | solution.py:30
  21.8 0.4 %all-to-all-done = f32[8,97,1,128]{3,2,1,0:T(1,128)S(1)} async-done(((f32[8,97,1,128]{3,2,1,0:T(1,128)}), f32[8,97,1,128]{3,2,1,0:T(1,128)S(1)}, u32[]{:S(2)}, u32[]{:S(2)}) %all-to-all-start) | async-done | bytes 397344 | tf_op jit(solution)/shard_map/all_to_all | solution.py:371
  22.2 1.0 %shard_map.134 = f32[32,1024]{1,0:T(8,128)} custom-call(bf16[32,128]{1,0:T(8,128)(2,1)S(1)} %copy-done.5, f32[32,1024]{1,0:T(8,128)S(1)} %get-tuple-element.11.adjoint_ref, f32[32,128]{1,0:T(8,128)S(1)} %collective-permute-done.1.rim_ref, f32[776,128]{1,0:T(8,128)S(1)} %bitcast.6, f32[64,128]{1,0:T(8,128)S(1)} %get-tuple-element.15.turned_ref, ...), custom_call_target="tpu_custom_call" | custom-call | tf_op jit(solution)/shard_map/pallas_call | solution.py:325
  (10 shorter events, 0.0 us)
Async XLA Ops:
  0.6 12.9 %copy-start.4 = (f32[3,6,1024]{2,1,0:T(8,128)S(1)}, f32[3,6,1024]{2,1,0:T(8,128)}, u32[]{:S(2)}) copy-start(f32[3,6,1024]{2,1,0:T(8,128)} %curl_ref.1) | copy-start | bytes 221188
  2.9 10.6 %copy-start = (f32[32,1024]{1,0:T(8,128)S(1)}, f32[32,1024]{1,0:T(8,128)}, u32[]{:S(2)}) copy-start(f32[32,1024]{1,0:T(8,128)} %coeffs_ref.1) | copy-start | bytes 393220
  2.9 10.6 %copy-start.1 = (bf16[6,32,1024]{2,1,0:T(8,128)(2,1)S(1)}, bf16[6,32,1024]{2,1,0:T(8,128)(2,1)}, u32[]{:S(2)}) copy-start(bf16[6,32,1024]{2,1,0:T(8,128)(2,1)} %jac_ref.1) | copy-start | bytes 1179652
  3.0 10.6 %copy-start.3 = (bf16[3,32,1024]{2,1,0:T(8,128)(2,1)S(1)}, bf16[3,32,1024]{2,1,0:T(8,128)(2,1)}, u32[]{:S(2)}) copy-start(bf16[3,32,1024]{2,1,0:T(8,128)(2,1)} %fwd_ref.1) | copy-start | bytes 589828
  3.0 10.6 %copy-start.5 = (bf16[32,128]{1,0:T(8,128)(2,1)S(1)}, bf16[32,128]{1,0:T(8,128)(2,1)}, u32[]{:S(2)}) copy-start(bf16[32,128]{1,0:T(8,128)(2,1)} %constant.7.clone.back_ref) | copy-start | bytes 24580
  3.0 10.6 %copy-start.6 = (s32[6,1024]{1,0:T(8,128)S(1)}, s32[6,1024]{1,0:T(8,128)}, u32[]{:S(2)}) copy-start(s32[6,1024]{1,0:T(8,128)} %edge_ref.1) | copy-start | bytes 73732
  3.0 10.6 %copy-start.7 = (bf16[32,128]{1,0:T(8,128)(2,1)S(1)}, bf16[32,128]{1,0:T(8,128)(2,1)}, u32[]{:S(2)}) copy-start(bf16[32,128]{1,0:T(8,128)(2,1)} %constant.6.clone.table_far.table_ref) | copy-start | bytes 24580
  3.0 10.6 %copy-start.9 = (f32[1024]{0:T(1024)S(1)}, f32[1024]{0:T(1024)}, u32[]{:S(2)}) copy-start(f32[1024]{0:T(1024)} %param.17) | copy-start | bytes 12292
  3.0 19.2 %all-to-all-start = ((f32[8,97,1,128]{3,2,1,0:T(1,128)}), f32[8,97,1,128]{3,2,1,0:T(1,128)S(1)}, u32[]{:S(2)}, u32[]{:S(2)}) async-start(f32[8,97,1,128]{3,2,1,0:T(1,128)} %bitcast.12), calls=%async_computation | async-start | bytes 794624 | tf_op jit(solution)/shard_map/all_to_all | solution.py:371
  10.5 3.1 %collective-permute-start = (f32[32,128]{1,0:T(8,128)S(1)}, f32[32,128]{1,0:T(8,128)S(1)}, u32[]{:S(2)}, u32[]{:S(2)}) collective-permute-start(f32[32,128]{1,0:T(8,128)S(1)} %get-tuple-element.10), channel_id=1, source_target_pairs={{1,0},{2,1},{3,2},{5,4},{6,5},{7,6},{9,8},{10,9},{11,10},{13,12},{... | collective-permute-start | bytes 49160 | tf_op jit(solution)/shard_map/ppermute | solution.py:30
  13.6 7.4 %copy-start.2 = (f32[128,128]{1,0:T(8,128)S(1)}, f32[128,128]{1,0:T(8,128)}, u32[]{:S(2)}) copy-start(f32[128,128]{1,0:T(8,128)} %mortar_ref.1) | copy-start | bytes 196612
  13.6 7.4 %copy-start.8 = (bf16[64,128]{1,0:T(8,128)(2,1)S(1)}, bf16[64,128]{1,0:T(8,128)(2,1)}, u32[]{:S(2)}) copy-start(bf16[64,128]{1,0:T(8,128)(2,1)} %constant.8.clone.wide_ref) | copy-start | bytes 49156
  16.8 4.2 %copy-start.10 = (s32[128,1]{0,1:T(1,128)S(1)}, s32[128,1]{0,1:T(1,128)}, u32[]{:S(2)}) copy-start(s32[128,1]{0,1:T(1,128)} %param.19) | copy-start | bytes 1540
  16.8 4.2 %copy-start.11 = (s32[128]{0:T(128)S(1)}, s32[128]{0:T(128)}, u32[]{:S(2)}) copy-start(s32[128]{0:T(128)} %param.20) | copy-start | bytes 1540
  16.8 5.0 %collective-permute-start.1 = (f32[32,128]{1,0:T(8,128)S(1)}, f32[32,128]{1,0:T(8,128)S(1)}, u32[]{:S(2)}, u32[]{:S(2)}) collective-permute-start(f32[32,128]{1,0:T(8,128)S(1)} %get-tuple-element.12.after_ref), channel_id=1, source_target_pairs={{0,1},{1,2},{2,3},{4,5},{5,6},{6,7},{8,9},{9,10},{10,11},{12,13},{... | collective-permute-start | bytes 49160 | tf_op jit(solution)/shard_map/ppermute | solution.py:30

commit v4 on v3

--- a/solution.py
+++ b/solution.py
@@ -16,6 +16,8 @@
 CHUNK = 256
 LOOK = (1, 3, 5)
 NEAR_BYTES = 1 << 20
+MOST_PERMUTES = 8
+
 
 PENALTY = 4.0
 SIMP_POWER = 3.0
@@ -68,19 +70,31 @@
     return lax.broadcasted_iota(jnp.int32, shape, dim)
 
 
+def by_permutes(stators):
+    return 4 <= stators <= MOST_PERMUTES and stators & (stators - 1) == 0
+
+
+def places_of(peer_ref, stators):
+    peers = peer_ref[...]
+    return peers ^ lax.axis_index("stator") if by_permutes(stators) else peers
+
+
 def triple(value):
     high, low = split(value)
     return jnp.concatenate([high, low, high], 1)
 
 
 def gap_kernel(
-    samples, stators, blocks, face, rotor_start, table_far, coeffs_far, mortar_far, peer_far, block_far,
-    send_ref, mapped_ref, rim_ref, table_ref, coeffs_ref, mortar_ref, peer_ref, block_ref, sems,
+    samples, stators, blocks, face, rotor_start, later, table_far, coeffs_far, mortar_far, peer_far, block_far, *refs,
 ):
+    later_far, (mapped_ref, rim_ref), refs = refs[:later], refs[later : later + 2], refs[later + 2 :]
+    later_near, refs = refs[:later], refs[later:]
+    *send_refs, table_ref, coeffs_ref, mortar_ref, peer_ref, block_ref, sems, later_sems = refs
     fars = (peer_far, block_far, coeffs_far, table_far, mortar_far)
     nears = (peer_ref, block_ref, coeffs_ref, table_ref, mortar_ref)
     copies = [pltpu.make_async_copy(far, near, sems.at[i]) for i, (far, near) in enumerate(zip(fars, nears))]
-    for copy in copies:
+    ahead = [pltpu.make_async_copy(far, near, later_sems.at[i]) for i, (far, near) in enumerate(zip(later_far, later_near))]
+    for copy in copies + ahead:
         copy.start()
     rows = samples * blocks
     slots = 2 * rows
@@ -93,7 +107,7 @@
     sample = (iota((1, rows), 1) % samples).astype(F32) + 1.0
     for copy in copies:
         copy.wait()
-    both = jnp.concatenate([peer_ref[...], block_ref[...]], 0).astype(F32)
+    both = jnp.concatenate([places_of(peer_ref, stators), block_ref[...]], 0).astype(F32)
     both = jnp.concatenate([both, jnp.zeros((6, rows), F32)], 0).astype(BF)
     both = dot(both, move)
     peers, chosen = both[0:1], both[1:2]
@@ -119,18 +133,53 @@
     packed = picked[:, :GE] + picked[:, GE:]
     key = chosen * samples + sample
     keys = dot_t(jnp.broadcast_to(key, (8, rows)).astype(BF), pick)
+    spots = send_spots(stators, face_rows, capacity)
     for p in range(stators):
-        first = p * (face_rows + capacity + 1)
-        send_ref[first : first + face_rows, :] = mapped
-        first += face_rows
-        send_ref[first : first + capacity, :] = packed[p * capacity : (p + 1) * capacity]
-        first += capacity
         start = p * capacity
         part = keys[:, start // LANES * LANES : (start // LANES + 1) * LANES]
         turn = (LANES - start % LANES) % LANES
         if turn:
             part = pltpu.roll(part, turn, 1)
-        send_ref[first : first + 1, :] = part[:1]
+        which, face_at, slot_at, key_at = spots[p]
+        if face_at is not None:
+            send_refs[which][face_at : face_at + face_rows, :] = mapped
+        send_refs[which][slot_at : slot_at + capacity, :] = packed[start : start + capacity]
+        send_refs[which][key_at : key_at + 1, :] = part[:1]
+    for copy in ahead:
+        copy.wait()
+
+
+def send_spots(stators, face_rows, capacity):
+    each = face_rows + capacity + 1
+    if not by_permutes(stators):
+        return [(0, p * each, p * each + face_rows, (p + 1) * each - 1) for p in range(stators)]
+    spots = [(0, 0, face_rows, each - 1), (1, 0, face_rows, each - 1)]
+    for p in range(2, stators, 2):
+        last = face_rows + 2 * capacity
+        spots.append((1 + p // 2, 0, face_rows, last))
+        spots.append((1 + p // 2, None, face_rows + capacity, last + 1))
+    return spots
+
+
+def got_spots(stators, face_rows, capacity):
+    each = face_rows + capacity + 1
+    spots = send_spots(stators, face_rows, capacity)
+    if by_permutes(stators):
+        for p in range(3, stators, 2):
+            base = (p - 3) // 2 * each
+            spots[p] = (1 + stators // 2, base, base + face_rows, base + each - 1)
+    return spots
+
+
+def relay_kernel(face_rows, capacity, *refs):
+    *got_refs, after_ref, out_ref = refs
+    each = face_rows + capacity + 1
+    last = face_rows + 2 * capacity + 1
+    for i, got_ref in enumerate(got_refs):
+        base = i * each
+        out_ref[base : base + face_rows, :] = got_ref[:face_rows, :]
+        out_ref[base + face_rows : base + each - 1, :] = got_ref[face_rows + capacity : last - 1, :]
+        out_ref[base + each - 1 : base + each, :] = got_ref[last : last + 1, :]
 
 
 def choose_kernel(
@@ -141,7 +190,7 @@
     turned_ref[...] = dot_t(triple(mapped_ref[...]), mortar_across)
     rows = samples * blocks
     pairs = stators * QB
-    wanted = (peer_ref[...] * QB + block_ref[...]).astype(F32)
+    wanted = (places_of(peer_ref, stators) * QB + block_ref[...]).astype(F32)
     wanted = jnp.broadcast_to(wanted, (8, rows)).astype(BF)
     lane = iota((rows, LANES), 1) % samples
     row = iota((rows, LANES), 0)
@@ -266,15 +315,19 @@
 
 
 def join_kernel(
-    samples, stators, blocks, face, rotor_start, back_ref, adjoint_ref, rim_ref, got_ref, turned_ref, choose_ref,
-    out_ref,
+    samples, stators, blocks, face, rotor_start, back_ref, adjoint_ref, rim_ref, turned_ref, choose_ref, *got_refs,
 ):
+    *got_refs, out_ref = got_refs
     slots = 2 * samples * blocks
     capacity = slots // stators
     face_rows = QB * samples
-    keys_at = face_rows + capacity
-    each = keys_at + 1
-    faces = jnp.concatenate([got_ref[p * each : p * each + face_rows, :] for p in range(stators)], 0)
+    spots = got_spots(stators, face_rows, capacity)
+
+    def got(p, part, count):
+        start = spots[p][part]
+        return got_refs[spots[p][0]][start : start + count, :]
+
+    faces = jnp.concatenate([got(p, 1, face_rows) for p in range(stators)], 0)
     face_high, face_low = split(faces)
     facing = dot(choose_ref[...], jnp.concatenate([face_high, face_low], 1))
     rows = blocks * samples
@@ -285,14 +338,14 @@
     for v in range(slots // LANES):
         acc = jnp.zeros((1, LANES), F32)
         for p in range(v * LANES // capacity, (v + 1) * LANES // capacity):
-            part = jnp.where(lane < capacity, got_ref[p * each + keys_at : (p + 1) * each, :], 0.0)
+            part = jnp.where(lane < capacity, got(p, 3, 1), 0.0)
             turn = p * capacity % LANES
             acc = acc + (pltpu.roll(part, turn, 1) if turn else part)
         key_parts.append(acc[0:1])
     key = jnp.concatenate(key_parts, 1)
     hit = jnp.where(key == (iota((face_rows, slots), 0) + 1).astype(F32), 1.0, 0.0)
     count = jnp.sum(hit, 1, keepdims=True)
-    packed = jnp.concatenate([got_ref[p * each + face_rows : p * each + keys_at, :] for p in range(stators)], 0)
+    packed = jnp.concatenate([got(p, 2, capacity) for p in range(stators)], 0)
     packed_high, packed_low = split(packed)
     gathered = dot(hit.astype(BF), jnp.concatenate([packed_high, packed_low], 1))
     gathered = (gathered[:, :GE] + gathered[:, GE:] - count * turned_ref[...]) * (-PENALTY)
@@ -355,27 +408,53 @@
     wide = jnp.asarray(np.tile(np.concatenate([wide_high, wide_low], 0), (1, LANES // samples)))
     peer = gap_peer.reshape(1, rows)
     block = gap_block.reshape(1, rows)
-    ahead = (table, coeffs, mortar, peer, block)
-    send, mapped, rim = call(
-        functools.partial(gap_kernel, samples, stators, blocks, face, rotor_start),
+    first = (table, coeffs, mortar, peer, block)
+    later = (coeffs, elem_edge, density.reshape(1, elements), curl_map, flux_fwd, jacobian)
+    each = face_rows + capacity + 1
+    permutes = by_permutes(stators)
+    if permutes:
+        sends = [(True, (each, GE), F32)] * 2 + [(True, (each + capacity + 1, GE), F32)] * (stators // 2 - 1)
+    else:
+        sends = [(False, (stators * each, GE), F32)]
+
+    def swapped(value, distance):
+        return lax.ppermute(value, "stator", [(i, i ^ distance) for i in range(stators)])
+
+    mapped, rim, *rest = call(
+        functools.partial(gap_kernel, samples, stators, blocks, face, rotor_start, len(later)),
         False,
-        (False, (stators * (face_rows + capacity + 1), GE), F32),
         (True, (face_rows, GE), F32),
         (True, (samples, face), F32),
-        far=ahead,
-        scratch=[pltpu.VMEM(value.shape, value.dtype) for value in ahead]
-        + [pltpu.SemaphoreType.DMA((len(ahead),))],
+        *[(True, value.shape, value.dtype) for value in later],
+        *sends,
+        far=first + later,
+        scratch=[pltpu.VMEM(value.shape, value.dtype) for value in first]
+        + [pltpu.SemaphoreType.DMA((len(first),)), pltpu.SemaphoreType.DMA((len(later),))],
     )()
+    later, send = rest[: len(later)], rest[len(later) :]
     rim = shifted(rim, "axial", -1)
-    parts = send.reshape(stators, face_rows + capacity + 1, 1, GE)
-    got = lax.all_to_all(parts, "stator", split_axis=0, concat_axis=0, tiled=True).reshape(send.shape)
+    if permutes:
+        got = [send[0]]
+        for i, value in enumerate(send[1:]):
+            distance = max(1, 2 * i)
+            got.append(swapped(value, distance))
+    else:
+        parts = send[0].reshape(stators, each, 1, GE)
+        got = lax.all_to_all(parts, "stator", split_axis=0, concat_axis=0, tiled=True)
+        got = [got.reshape(stators * each, GE)]
+    own, edge, weight, curl, fwd, jac = later
     adjoint, rim_out, grad = call(
         functools.partial(element_kernel, face, rotor_start),
         True,
         (True, (samples, edges), F32),
         (True, (samples, face), F32),
         (False, (1, elements), F32),
-    )(table, back, coeffs, rim, elem_edge, curl_map, jacobian, flux_fwd, density.reshape(1, elements))
+    )(table, back, own, rim, edge, curl, jac, fwd, weight)
+    if permutes:
+        (send,) = call(
+            functools.partial(relay_kernel, face_rows, capacity), True, (True, ((stators // 2 - 1) * each, GE), F32)
+        )(*got[2:], rim_out)
+        got.append(swapped(send, 1))
     lower = shifted(rim_out, "axial", 1)
     choose, turned = call(
         functools.partial(choose_kernel, samples, stators, blocks),
@@ -387,7 +466,7 @@
         functools.partial(join_kernel, samples, stators, blocks, face, rotor_start),
         True,
         (False, (samples, edges), F32),
-    )(back, adjoint, lower, got, turned, choose)
+    )(back, adjoint, lower, turned, choose, *got)
     return adjoint, grad.reshape(elements)
 
 

time: 23.6 us -> 23 us (0.975)
  the two profiles are of different devices: /device:TPU:0 before, /device:TPU:1 now
where the time goes in v4:
time: 23 us; the launch traced here: 22.8 us
  starting transfers between devices  11.3 us (49%)
  Pallas kernels  6.22 us (27%)
  waiting for transfers between devices  4.51 us (20%)
  between operations  0.74 us (3%)
    pallas_call x5, Pallas kernels, run(): pl.pallas_call(kernel, out_shape=[pltpu.VMEM(shape, kind) if inside and s...  6.22 us
    ppermute x5, starting transfers between devices, swapped(): lax.ppermute(value, 'stator', [(i, i ^ distance) for i in range(stators)])  6.02 us
    ppermute x2, starting transfers between devices, shifted(): lax.ppermute(value, axis, [(source, source + steps) for source in range(l...  5.32 us
    ppermute x2, waiting for transfers between devices, shifted(): lax.ppermute(value, axis, [(source, source + steps) for source in range(l...  3.62 us
    ppermute x5, waiting for transfers between devices, swapped(): lax.ppermute(value, 'stator', [(i, i ^ distance) for i in range(stators)])  0.89 us
  transfers between devices with their start and end apart: 7, of which 3 were waited for; matrix products, arithmetic and copies ran while one was open for 0% of the time, Pallas kernels for 15%

profile of v4, /device:TPU:1, one launch (start us, length us, event | category | flops | bytes accessed | tf_op | source)
XLA Modules:
  0.0 22.8 jit_solution(3570662765380289507)
XLA Ops:
  0.6 1.8 %shard_map.131 = (f32[64,128]{1,0:T(8,128)S(1)}, f32[32,128]{1,0:T(8,128)S(1)}, f32[32,1024]{1,0:T(8,128)S(1)}, s32[6,1024]{1,0:T(8,128)S(1)}, f32[1,1024]{1,0:T...) custom-call(bf16[32,128]{1,0:T(8,128)(2,1)} %constant.6.clone.table_, ...), custom_call_target="tpu_custom_call" | custom-call | tf_op jit(solution)/shard_map/pallas_call | solution.py:378
  2.4 2.2 %collective-permute-start.3 = (f32[130,128]{1,0:T(8,128)S(1)}, f32[130,128]{1,0:T(8,128)S(1)}, u32[]{:S(2)}, u32[]{:S(2)}) collective-permute-start(f32[130,128]{1,0:T(8,128)S(1)} %get-tuple-element.34), channel_id=1, source_target_pairs={{0,8},{4,12},{8,0},{12,4},{16,24},{20,28},{24,16},{28,20},{1,9},{5... | collective-permute-start | bytes 199688 | tf_op jit(solution)/shard_map/ppermute | solution.py:421
  4.6 2.3 %collective-permute-start.4 = (f32[130,128]{1,0:T(8,128)S(1)}, f32[130,128]{1,0:T(8,128)S(1)}, u32[]{:S(2)}, u32[]{:S(2)}) collective-permute-start(f32[130,128]{1,0:T(8,128)S(1)} %get-tuple-element.35), channel_id=1, source_target_pairs={{0,16},{4,20},{8,24},{12,28},{16,0},{20,4},{24,8},{28,12},{1,17},{... | collective-permute-start | bytes 199688 | tf_op jit(solution)/shard_map/ppermute | solution.py:421
  6.9 0.0 collective-permute-start.5
  6.9 3.1 %collective-permute-start = (f32[32,128]{1,0:T(8,128)S(1)}, f32[32,128]{1,0:T(8,128)S(1)}, u32[]{:S(2)}, u32[]{:S(2)}) collective-permute-start(f32[32,128]{1,0:T(8,128)S(1)} %get-tuple-element.21), channel_id=1, source_target_pairs={{1,0},{2,1},{3,2},{5,4},{6,5},{7,6},{9,8},{10,9},{11,10},{13,12},{... | collective-permute-start | bytes 49160 | tf_op jit(solution)/shard_map/ppermute | solution.py:32
  10.1 3.0 %collective-permute-done.rim_ref = f32[32,128]{1,0:T(8,128)S(1)} collective-permute-done((f32[32,128]{1,0:T(8,128)S(1)}, f32[32,128]{1,0:T(8,128)S(1)}, u32[]{:S(2)}, u32[]{:S(2)}) %collective-permute-start) | collective-permute-done | bytes 16416 | tf_op jit(solution)/shard_map/ppermute | solution.py:32
  13.1 0.0 copy-done.2
  13.1 0.0 copy-done.1
  13.1 3.1 %shard_map.132 = (f32[32,1024]{1,0:T(8,128)S(1)}, f32[32,128]{1,0:T(8,128)S(1)}, f32[1,1024]{1,0:T(1,128)}) custom-call(bf16[32,128]{1,0:T(8,128)(2,1)S(1)} %copy-done.2, bf16[32,128]{1,0:T(8,128)(2,1)S(1)} %copy-done.1, f32[32,1024]{1,0:T(8,128)S(1)} %get-tuple-element.20.coeffs_ref, f32[32,128]{1,0:T(8,128)S(1)} %collective-permute-done.rim_ref, ...), custom_call_target="tpu_custom_call" | custom-call | tf_op jit(solution)/shard_map/pallas_call | solution.py:378
  16.2 0.0 collective-permute-done.3.refs_0_.got_refs_2_
  16.2 0.0 collective-permute-done.4.refs_1_.got_refs_3_
  16.3 0.0 collective-permute-done.5.refs_2_.got_refs_4_
  16.3 0.0 copy-start
  16.3 0.0 copy-start.3
  16.3 1.3 %collective-permute-start.6 = (f32[291,128]{1,0:T(8,128)S(1)}, f32[291,128]{1,0:T(8,128)S(1)}, u32[]{:S(2)}, u32[]{:S(2)}) collective-permute-start(f32[291,128]{1,0:T(8,128)S(1)} %shard_map.134), channel_id=1, source_target_pairs={{0,4},{4,0},{8,12},{12,8},{16,20},{20,16},{24,28},{28,24},{1,5},{5... | collective-permute-start | bytes 446984 | tf_op jit(solution)/shard_map/ppermute | solution.py:421
  17.6 0.2 collective-permute-start.2
  17.9 2.2 %collective-permute-start.1 = (f32[32,128]{1,0:T(8,128)S(1)}, f32[32,128]{1,0:T(8,128)S(1)}, u32[]{:S(2)}, u32[]{:S(2)}) collective-permute-start(f32[32,128]{1,0:T(8,128)S(1)} %get-tuple-element.28.after_ref.refs_3_), channel_id=1, source_target_pairs={{0,1},{1,2},{2,3},{4,5},{5,6},{6,7},{8,9},{9,10},{10,11},{12,13},{... | collective-permute-start | bytes 49160 | tf_op jit(solution)/shard_map/ppermute | solution.py:32
  20.0 0.0 copy-done
  20.1 0.0 copy-done.3
  20.1 0.2 shard_map.133
  20.3 0.6 %collective-permute-done.1.rim_ref = f32[32,128]{1,0:T(8,128)S(1)} collective-permute-done((f32[32,128]{1,0:T(8,128)S(1)}, f32[32,128]{1,0:T(8,128)S(1)}, u32[]{:S(2)}, u32[]{:S(2)}) %collective-permute-start.1) | collective-permute-done | bytes 16416 | tf_op jit(solution)/shard_map/ppermute | solution.py:32
  20.9 0.9 %collective-permute-done.2.got_refs_1_ = f32[97,128]{1,0:T(8,128)S(1)} collective-permute-done((f32[97,128]{1,0:T(8,128)S(1)}, f32[97,128]{1,0:T(8,128)S(1)}, u32[]{:S(2)}, u32[]{:S(2)}) %collective-permute-start.2) | collective-permute-done | bytes 49696 | tf_op jit(solution)/shard_map/ppermute | solution.py:421
  21.8 0.0 collective-permute-done.6.got_refs_5_
  21.8 1.1 %shard_map.135 = f32[32,1024]{1,0:T(8,128)} custom-call(bf16[32,128]{1,0:T(8,128)(2,1)S(1)} %copy-done.1, f32[32,1024]{1,0:T(8,128)S(1)} %get-tuple-element.27.adjoint_ref, f32[32,128]{1,0:T(8,128)S(1)} %collective-permute-done.1.rim_ref, f32[64,128]{1,0:T(8,128)S(1)} %get-tuple-element.30.turned_ref, bf16[256,512]{1,0:T(8,128)(2,1)S(1)} %get-tuple-element.31.choose_ref, ...), custom_call_target="tpu_custom_call" | custom-call | tf_op jit(solution)/shard_map/pallas_call | solution.py:378
  (7 shorter events, 0.0 us)
Async XLA Ops:
  2.4 13.8 %collective-permute-start.3 = (f32[130,128]{1,0:T(8,128)S(1)}, f32[130,128]{1,0:T(8,128)S(1)}, u32[]{:S(2)}, u32[]{:S(2)}) collective-permute-start(f32[130,128]{1,0:T(8,128)S(1)} %get-tuple-element.34), channel_id=1, source_target_pairs={{0,8},{4,12},{8,0},{12,4},{16,24},{20,28},{24,16},{28,20},{1,9},{5... | collective-permute-start | bytes 199688 | tf_op jit(solution)/shard_map/ppermute | solution.py:421
  4.6 8.5 %copy-start.2 = (bf16[32,128]{1,0:T(8,128)(2,1)S(1)}, bf16[32,128]{1,0:T(8,128)(2,1)}, u32[]{:S(2)}) copy-start(bf16[32,128]{1,0:T(8,128)(2,1)} %constant.6.clone.table_far.table_ref) | copy-start | bytes 24580
  4.6 8.5 %copy-start.1 = (bf16[32,128]{1,0:T(8,128)(2,1)S(1)}, bf16[32,128]{1,0:T(8,128)(2,1)}, u32[]{:S(2)}) copy-start(bf16[32,128]{1,0:T(8,128)(2,1)} %constant.7.clone.back_ref) | copy-start | bytes 24580
  4.6 11.6 %collective-permute-start.4 = (f32[130,128]{1,0:T(8,128)S(1)}, f32[130,128]{1,0:T(8,128)S(1)}, u32[]{:S(2)}, u32[]{:S(2)}) collective-permute-start(f32[130,128]{1,0:T(8,128)S(1)} %get-tuple-element.35), channel_id=1, source_target_pairs={{0,16},{4,20},{8,24},{12,28},{16,0},{20,4},{24,8},{28,12},{1,17},{... | collective-permute-start | bytes 199688 | tf_op jit(solution)/shard_map/ppermute | solution.py:421
  6.9 9.3 %collective-permute-start.5 = (f32[130,128]{1,0:T(8,128)S(1)}, f32[130,128]{1,0:T(8,128)S(1)}, u32[]{:S(2)}, u32[]{:S(2)}) collective-permute-start(f32[130,128]{1,0:T(8,128)S(1)} %get-tuple-element.36), channel_id=1, source_target_pairs={{0,24},{4,28},{8,16},{12,20},{16,8},{20,12},{24,0},{28,4},{1,25},{... | collective-permute-start | bytes 199688 | tf_op jit(solution)/shard_map/ppermute | solution.py:421
  6.9 6.2 %collective-permute-start = (f32[32,128]{1,0:T(8,128)S(1)}, f32[32,128]{1,0:T(8,128)S(1)}, u32[]{:S(2)}, u32[]{:S(2)}) collective-permute-start(f32[32,128]{1,0:T(8,128)S(1)} %get-tuple-element.21), channel_id=1, source_target_pairs={{1,0},{2,1},{3,2},{5,4},{6,5},{7,6},{9,8},{10,9},{11,10},{13,12},{... | collective-permute-start | bytes 49160 | tf_op jit(solution)/shard_map/ppermute | solution.py:32
  16.3 3.8 %copy-start = (f32[128,128]{1,0:T(8,128)S(1)}, f32[128,128]{1,0:T(8,128)}, u32[]{:S(2)}) copy-start(f32[128,128]{1,0:T(8,128)} %mortar_ref.1) | copy-start | bytes 196612
  16.3 3.8 %copy-start.3 = (bf16[64,128]{1,0:T(8,128)(2,1)S(1)}, bf16[64,128]{1,0:T(8,128)(2,1)}, u32[]{:S(2)}) copy-start(bf16[64,128]{1,0:T(8,128)(2,1)} %constant.8.clone.wide_ref) | copy-start | bytes 49156
  16.3 5.5 %collective-permute-start.6 = (f32[291,128]{1,0:T(8,128)S(1)}, f32[291,128]{1,0:T(8,128)S(1)}, u32[]{:S(2)}, u32[]{:S(2)}) collective-permute-start(f32[291,128]{1,0:T(8,128)S(1)} %shard_map.134), channel_id=1, source_target_pairs={{0,4},{4,0},{8,12},{12,8},{16,20},{20,16},{24,28},{28,24},{1,5},{5... | collective-permute-start | bytes 446984 | tf_op jit(solution)/shard_map/ppermute | solution.py:421
  17.6 2.4 %copy-start.4 = (s32[128,1]{0,1:T(1,128)S(1)}, s32[128,1]{0,1:T(1,128)}, u32[]{:S(2)}) copy-start(s32[128,1]{0,1:T(1,128)} %param.19) | copy-start | bytes 1540
  17.6 2.5 %copy-start.5 = (s32[128]{0:T(128)S(1)}, s32[128]{0:T(128)}, u32[]{:S(2)}) copy-start(s32[128]{0:T(128)} %param.20) | copy-start | bytes 1540
  17.6 4.2 %collective-permute-start.2 = (f32[97,128]{1,0:T(8,128)S(1)}, f32[97,128]{1,0:T(8,128)S(1)}, u32[]{:S(2)}, u32[]{:S(2)}) collective-permute-start(f32[97,128]{1,0:T(8,128)S(1)} %get-tuple-element.33), channel_id=1, source_target_pairs={{0,4},{4,0},{8,12},{12,8},{16,20},{20,16},{24,28},{28,24},{1,5},{5... | collective-permute-start | bytes 149000 | tf_op jit(solution)/shard_map/ppermute | solution.py:421
  17.9 3.1 %collective-permute-start.1 = (f32[32,128]{1,0:T(8,128)S(1)}, f32[32,128]{1,0:T(8,128)S(1)}, u32[]{:S(2)}, u32[]{:S(2)}) collective-permute-start(f32[32,128]{1,0:T(8,128)S(1)} %get-tuple-element.28.after_ref.refs_3_), channel_id=1, source_target_pairs={{0,1},{1,2},{2,3},{4,5},{5,6},{6,7},{8,9},{9,10},{10,11},{12,13},{... | collective-permute-start | bytes 49160 | tf_op jit(solution)/shard_map/ppermute | solution.py:32

commit v5 on v4

--- a/solution.py
+++ b/solution.py
@@ -14,7 +14,7 @@
 LANES = 128
 WIDE = 256
 CHUNK = 256
-LOOK = (1, 3, 5)
+LOOK = (3, 5)
 NEAR_BYTES = 1 << 20
 MOST_PERMUTES = 8
 
@@ -228,7 +228,8 @@
     )
     places = iota((WIDE, LANES), 0).astype(F32).astype(BF)
     summed = jnp.zeros((wides * 2 * samples, WIDE), F32)
-    for chunk in range(elements // CHUNK):
+
+    def prepare(chunk):
         lane_slices = [
             slice(chunk * CHUNK + half * LANES, chunk * CHUNK + (half + 1) * LANES) for half in range(CHUNK // LANES)
         ]
@@ -242,6 +243,15 @@
                 parts.append(jnp.where(place == places, jnp.ones_like(place), jnp.zeros_like(place)))
             rights.append(jnp.concatenate(parts, 1))
         looked = {m: dot(stack, rights[m]) for m in LOOK}
+        return lane_slices, rights, looked
+
+    chunks = elements // CHUNK
+    ready = [prepare(chunk) for chunk in range(min(1, chunks))]
+    waiting = []
+    for chunk in range(chunks):
+        if chunk + 1 < chunks and 1:
+            ready.append(prepare(chunk + 1))
+        lane_slices, rights, looked = ready[chunk]
         left_lanes = [[] for _ in range(6)]
         for half, lanes in enumerate(lane_slices):
             at = slice(half * LANES, (half + 1) * LANES)
@@ -300,7 +310,10 @@
                     jnp.concatenate([jnp.where(wide == w, pair, jnp.zeros_like(pair)) for w in range(wides)], 0)
                 )
         left = jnp.concatenate([part for m in range(6) for part in left_lanes[m]], 1)
-        summed = summed + dot_t(left, jnp.concatenate(rights, 1))
+        waiting.append((left, jnp.concatenate(rights, 1)))
+        if chunk:
+            summed = summed + dot_t(*waiting[chunk - 1])
+    summed = summed + dot_t(*waiting[-1])
     pieces = []
     for w in range(wides):
         base = w * 2 * samples

time: 23 us -> 23 us (level)
  transfers between devices with their start and end apart: 7 -> 7, of which waited for: 3 -> 3; matrix products, arithmetic and copies ran while one was open for 0% -> 0% of each run, Pallas kernels for 15% -> 14%
where the time goes in v5:
time: 23 us; the launch traced here: 22.8 us
  starting transfers between devices  11.3 us (49%)
  Pallas kernels  6.12 us (27%)
  waiting for transfers between devices  4.56 us (20%)
  between operations  0.73 us (3%)
    pallas_call x5, Pallas kernels, run(): pl.pallas_call(kernel, out_shape=[pltpu.VMEM(shape, kind) if inside and s...  6.12 us
    ppermute x5, starting transfers between devices, swapped(): lax.ppermute(value, 'stator', [(i, i ^ distance) for i in range(stators)])  6.02 us
    ppermute x2, starting transfers between devices, shifted(): lax.ppermute(value, axis, [(source, source + steps) for source in range(l...  5.32 us
    ppermute x2, waiting for transfers between devices, shifted(): lax.ppermute(value, axis, [(source, source + steps) for source in range(l...  3.62 us
    ppermute x5, waiting for transfers between devices, swapped(): lax.ppermute(value, 'stator', [(i, i ^ distance) for i in range(stators)])  0.94 us
  transfers between devices with their start and end apart: 7, of which 3 were waited for; matrix products, arithmetic and copies ran while one was open for 0% of the time, Pallas kernels for 14%

profile of v5, /device:TPU:1, one launch (start us, length us, event | category | flops | bytes accessed | tf_op | source)
XLA Modules:
  0.0 22.8 jit_solution(5582929495874546359)
XLA Ops:
  0.6 1.8 %shard_map.131 = (f32[64,128]{1,0:T(8,128)S(1)}, f32[32,128]{1,0:T(8,128)S(1)}, f32[32,1024]{1,0:T(8,128)S(1)}, s32[6,1024]{1,0:T(8,128)S(1)}, f32[1,1024]{1,0:T...) custom-call(bf16[32,128]{1,0:T(8,128)(2,1)} %constant.6.clone.table_, ...), custom_call_target="tpu_custom_call" | custom-call | tf_op jit(solution)/shard_map/pallas_call | solution.py:391
  2.4 2.2 %collective-permute-start.3 = (f32[130,128]{1,0:T(8,128)S(1)}, f32[130,128]{1,0:T(8,128)S(1)}, u32[]{:S(2)}, u32[]{:S(2)}) collective-permute-start(f32[130,128]{1,0:T(8,128)S(1)} %get-tuple-element.34), channel_id=1, source_target_pairs={{0,8},{4,12},{8,0},{12,4},{16,24},{20,28},{24,16},{28,20},{1,9},{5... | collective-permute-start | bytes 199688 | tf_op jit(solution)/shard_map/ppermute | solution.py:434
  4.6 2.3 %collective-permute-start.4 = (f32[130,128]{1,0:T(8,128)S(1)}, f32[130,128]{1,0:T(8,128)S(1)}, u32[]{:S(2)}, u32[]{:S(2)}) collective-permute-start(f32[130,128]{1,0:T(8,128)S(1)} %get-tuple-element.35), channel_id=1, source_target_pairs={{0,16},{4,20},{8,24},{12,28},{16,0},{20,4},{24,8},{28,12},{1,17},{... | collective-permute-start | bytes 199688 | tf_op jit(solution)/shard_map/ppermute | solution.py:434
  6.9 0.0 collective-permute-start.5
  6.9 3.1 %collective-permute-start = (f32[32,128]{1,0:T(8,128)S(1)}, f32[32,128]{1,0:T(8,128)S(1)}, u32[]{:S(2)}, u32[]{:S(2)}) collective-permute-start(f32[32,128]{1,0:T(8,128)S(1)} %get-tuple-element.21), channel_id=1, source_target_pairs={{1,0},{2,1},{3,2},{5,4},{6,5},{7,6},{9,8},{10,9},{11,10},{13,12},{... | collective-permute-start | bytes 49160 | tf_op jit(solution)/shard_map/ppermute | solution.py:32
  10.1 3.0 %collective-permute-done.rim_ref = f32[32,128]{1,0:T(8,128)S(1)} collective-permute-done((f32[32,128]{1,0:T(8,128)S(1)}, f32[32,128]{1,0:T(8,128)S(1)}, u32[]{:S(2)}, u32[]{:S(2)}) %collective-permute-start) | collective-permute-done | bytes 16416 | tf_op jit(solution)/shard_map/ppermute | solution.py:32
  13.1 0.0 copy-done.2
  13.1 0.0 copy-done.1
  13.1 3.0 %shard_map.132 = (f32[32,1024]{1,0:T(8,128)S(1)}, f32[32,128]{1,0:T(8,128)S(1)}, f32[1,1024]{1,0:T(1,128)}) custom-call(bf16[32,128]{1,0:T(8,128)(2,1)S(1)} %copy-done.2, bf16[32,128]{1,0:T(8,128)(2,1)S(1)} %copy-done.1, f32[32,1024]{1,0:T(8,128)S(1)} %get-tuple-element.20.coeffs_ref, f32[32,128]{1,0:T(8,128)S(1)} %collective-permute-done.rim_ref, ...), custom_call_target="tpu_custom_call" | custom-call | tf_op jit(solution)/shard_map/pallas_call | solution.py:391
  16.1 0.0 collective-permute-done.3.refs_0_.got_refs_2_
  16.1 0.0 collective-permute-done.4.refs_1_.got_refs_3_
  16.1 0.0 collective-permute-done.5.refs_2_.got_refs_4_
  16.1 0.0 copy-start
  16.2 0.0 copy-start.3
  16.2 1.3 %collective-permute-start.6 = (f32[291,128]{1,0:T(8,128)S(1)}, f32[291,128]{1,0:T(8,128)S(1)}, u32[]{:S(2)}, u32[]{:S(2)}) collective-permute-start(f32[291,128]{1,0:T(8,128)S(1)} %shard_map.134), channel_id=1, source_target_pairs={{0,4},{4,0},{8,12},{12,8},{16,20},{20,16},{24,28},{28,24},{1,5},{5... | collective-permute-start | bytes 446984 | tf_op jit(solution)/shard_map/ppermute | solution.py:434
  17.5 0.2 collective-permute-start.2
  17.7 2.2 %collective-permute-start.1 = (f32[32,128]{1,0:T(8,128)S(1)}, f32[32,128]{1,0:T(8,128)S(1)}, u32[]{:S(2)}, u32[]{:S(2)}) collective-permute-start(f32[32,128]{1,0:T(8,128)S(1)} %get-tuple-element.28.after_ref.refs_3_), channel_id=1, source_target_pairs={{0,1},{1,2},{2,3},{4,5},{5,6},{6,7},{8,9},{9,10},{10,11},{12,13},{... | collective-permute-start | bytes 49160 | tf_op jit(solution)/shard_map/ppermute | solution.py:32
  19.9 0.0 copy-done
  19.9 0.0 copy-done.3
  20.0 0.2 shard_map.133
  20.2 0.6 %collective-permute-done.1.rim_ref = f32[32,128]{1,0:T(8,128)S(1)} collective-permute-done((f32[32,128]{1,0:T(8,128)S(1)}, f32[32,128]{1,0:T(8,128)S(1)}, u32[]{:S(2)}, u32[]{:S(2)}) %collective-permute-start.1) | collective-permute-done | bytes 16416 | tf_op jit(solution)/shard_map/ppermute | solution.py:32
  20.8 0.9 %collective-permute-done.2.got_refs_1_ = f32[97,128]{1,0:T(8,128)S(1)} collective-permute-done((f32[97,128]{1,0:T(8,128)S(1)}, f32[97,128]{1,0:T(8,128)S(1)}, u32[]{:S(2)}, u32[]{:S(2)}) %collective-permute-start.2) | collective-permute-done | bytes 49696 | tf_op jit(solution)/shard_map/ppermute | solution.py:434
  21.7 0.0 collective-permute-done.6.got_refs_5_
  21.7 1.1 %shard_map.135 = f32[32,1024]{1,0:T(8,128)} custom-call(bf16[32,128]{1,0:T(8,128)(2,1)S(1)} %copy-done.1, f32[32,1024]{1,0:T(8,128)S(1)} %get-tuple-element.27.adjoint_ref, f32[32,128]{1,0:T(8,128)S(1)} %collective-permute-done.1.rim_ref, f32[64,128]{1,0:T(8,128)S(1)} %get-tuple-element.30.turned_ref, bf16[256,512]{1,0:T(8,128)(2,1)S(1)} %get-tuple-element.31.choose_ref, ...), custom_call_target="tpu_custom_call" | custom-call | tf_op jit(solution)/shard_map/pallas_call | solution.py:391
  (7 shorter events, 0.0 us)
Async XLA Ops:
  2.4 13.7 %collective-permute-start.3 = (f32[130,128]{1,0:T(8,128)S(1)}, f32[130,128]{1,0:T(8,128)S(1)}, u32[]{:S(2)}, u32[]{:S(2)}) collective-permute-start(f32[130,128]{1,0:T(8,128)S(1)} %get-tuple-element.34), channel_id=1, source_target_pairs={{0,8},{4,12},{8,0},{12,4},{16,24},{20,28},{24,16},{28,20},{1,9},{5... | collective-permute-start | bytes 199688 | tf_op jit(solution)/shard_map/ppermute | solution.py:434
  4.6 8.5 %copy-start.2 = (bf16[32,128]{1,0:T(8,128)(2,1)S(1)}, bf16[32,128]{1,0:T(8,128)(2,1)}, u32[]{:S(2)}) copy-start(bf16[32,128]{1,0:T(8,128)(2,1)} %constant.6.clone.table_far.table_ref) | copy-start | bytes 24580
  4.6 8.5 %copy-start.1 = (bf16[32,128]{1,0:T(8,128)(2,1)S(1)}, bf16[32,128]{1,0:T(8,128)(2,1)}, u32[]{:S(2)}) copy-start(bf16[32,128]{1,0:T(8,128)(2,1)} %constant.7.clone.back_ref) | copy-start | bytes 24580
  4.6 11.5 %collective-permute-start.4 = (f32[130,128]{1,0:T(8,128)S(1)}, f32[130,128]{1,0:T(8,128)S(1)}, u32[]{:S(2)}, u32[]{:S(2)}) collective-permute-start(f32[130,128]{1,0:T(8,128)S(1)} %get-tuple-element.35), channel_id=1, source_target_pairs={{0,16},{4,20},{8,24},{12,28},{16,0},{20,4},{24,8},{28,12},{1,17},{... | collective-permute-start | bytes 199688 | tf_op jit(solution)/shard_map/ppermute | solution.py:434
  6.9 9.2 %collective-permute-start.5 = (f32[130,128]{1,0:T(8,128)S(1)}, f32[130,128]{1,0:T(8,128)S(1)}, u32[]{:S(2)}, u32[]{:S(2)}) collective-permute-start(f32[130,128]{1,0:T(8,128)S(1)} %get-tuple-element.36), channel_id=1, source_target_pairs={{0,24},{4,28},{8,16},{12,20},{16,8},{20,12},{24,0},{28,4},{1,25},{... | collective-permute-start | bytes 199688 | tf_op jit(solution)/shard_map/ppermute | solution.py:434
  6.9 6.2 %collective-permute-start = (f32[32,128]{1,0:T(8,128)S(1)}, f32[32,128]{1,0:T(8,128)S(1)}, u32[]{:S(2)}, u32[]{:S(2)}) collective-permute-start(f32[32,128]{1,0:T(8,128)S(1)} %get-tuple-element.21), channel_id=1, source_target_pairs={{1,0},{2,1},{3,2},{5,4},{6,5},{7,6},{9,8},{10,9},{11,10},{13,12},{... | collective-permute-start | bytes 49160 | tf_op jit(solution)/shard_map/ppermute | solution.py:32
  16.1 3.8 %copy-start = (f32[128,128]{1,0:T(8,128)S(1)}, f32[128,128]{1,0:T(8,128)}, u32[]{:S(2)}) copy-start(f32[128,128]{1,0:T(8,128)} %mortar_ref.1) | copy-start | bytes 196612
  16.2 3.8 %copy-start.3 = (bf16[64,128]{1,0:T(8,128)(2,1)S(1)}, bf16[64,128]{1,0:T(8,128)(2,1)}, u32[]{:S(2)}) copy-start(bf16[64,128]{1,0:T(8,128)(2,1)} %constant.8.clone.wide_ref) | copy-start | bytes 49156
  16.2 5.5 %collective-permute-start.6 = (f32[291,128]{1,0:T(8,128)S(1)}, f32[291,128]{1,0:T(8,128)S(1)}, u32[]{:S(2)}, u32[]{:S(2)}) collective-permute-start(f32[291,128]{1,0:T(8,128)S(1)} %shard_map.134), channel_id=1, source_target_pairs={{0,4},{4,0},{8,12},{12,8},{16,20},{20,16},{24,28},{28,24},{1,5},{5... | collective-permute-start | bytes 446984 | tf_op jit(solution)/shard_map/ppermute | solution.py:434
  17.5 2.4 %copy-start.4 = (s32[128,1]{0,1:T(1,128)S(1)}, s32[128,1]{0,1:T(1,128)}, u32[]{:S(2)}) copy-start(s32[128,1]{0,1:T(1,128)} %param.19) | copy-start | bytes 1540
  17.5 2.5 %copy-start.5 = (s32[128]{0:T(128)S(1)}, s32[128]{0:T(128)}, u32[]{:S(2)}) copy-start(s32[128]{0:T(128)} %param.20) | copy-start | bytes 1540
  17.5 4.2 %collective-permute-start.2 = (f32[97,128]{1,0:T(8,128)S(1)}, f32[97,128]{1,0:T(8,128)S(1)}, u32[]{:S(2)}, u32[]{:S(2)}) collective-permute-start(f32[97,128]{1,0:T(8,128)S(1)} %get-tuple-element.33), channel_id=1, source_target_pairs={{0,4},{4,0},{8,12},{12,8},{16,20},{20,16},{24,28},{28,24},{1,5},{5... | collective-permute-start | bytes 149000 | tf_op jit(solution)/shard_map/ppermute | solution.py:434
  17.7 3.1 %collective-permute-start.1 = (f32[32,128]{1,0:T(8,128)S(1)}, f32[32,128]{1,0:T(8,128)S(1)}, u32[]{:S(2)}, u32[]{:S(2)}) collective-permute-start(f32[32,128]{1,0:T(8,128)S(1)} %get-tuple-element.28.after_ref.refs_3_), channel_id=1, source_target_pairs={{0,1},{1,2},{2,3},{4,5},{5,6},{6,7},{8,9},{9,10},{10,11},{12,13},{... | collective-permute-start | bytes 49160 | tf_op jit(solution)/shard_map/ppermute | solution.py:32
